TPU v7x, 128 devices: a whole 4x4x4 slice. The times are simulated.
128 devices in a mesh: rows: 2 (over core), cols: 64 (over z, y, x).
Axes of the slice: x: 4, y: 4, z: 4, core: 2. Of those that a mesh axis runs over, the one named last changes fastest.
Arguments:
- wind_speed: float32 [16, 8192], P('rows', 'cols'), may hold values from 3 to 25
- wind_dir: float32 [16, 8192], P('rows', 'cols'), may hold values from -3.140625 to 3.140625
- depth_class: int32 [16, 8192], P('rows', 'cols'), may hold values from 0 to 3
- group_speed: float32 [4, 24], replicated, may hold values from 0.3 to 3
- dissipation: float32 [4, 24], replicated, may hold values from 0.02 to 1
- input_rate: float32 [24], replicated, may hold values from 0.02 to 0.2
- outer_spectra: float32 [131072, 864], P(('rows', 'cols')), may hold values from -6 to 6
- dest_cell: int32 [131072], P(('rows', 'cols')), may hold values from 0 to 131071, as said below
- refraction_inverse: float32 [4, 216, 216], replicated, as said below
- sweep_order: int32 [2, 4], replicated, may hold values from 0 to 3, as said below
Outputs:
- wave_action: float32 [864, 16, 8192], P(None, 'rows', 'cols')
Inputs may be any that keep to these rules, and one draw needn't show every extreme that they name: `dest_cell`: every boundary point feeds a cell on the grid's outermost rows or columns. Among the points held by one device, at most 16 feed cells held by any one device, and in every draw one device receives exactly 16 points from every device. `refraction_inverse`: each matrix has a diagonal between 0.75 and 1 and off-diagonal entries below 1.2 / 216 in magnitude. `sweep_order`: each row names each of the four quadrants once.
All inputs are finite; a program needn't handle non-finite values.
Results may differ from a plain program's by a relative error of at most 0.0003.
Values sent between devices are 32-bit elements; how exact they have to be, the bound alone decides.
A program may use at most 192 MiB of HBM per device.

v0:
```python
from functools import partial
import math

import jax
import jax.numpy as jnp
import numpy as np
from jax import lax
from jax.experimental import pallas as pl
from jax.experimental.pallas import tpu as pltpu
from jax.sharding import PartitionSpec as P

NDIR = 36
NFREQ = 24
CAP = 16
ITERS = 2
QUARTER = NDIR // 4
KQ = QUARTER * NFREQ
KP = 256
K = 4 * KQ
KW = 896
ROWS = 16
HALF = 64
CW = 72

whitecap_rate = 0.5


def pack_kernel(source_ref, points_ref, cell_ref, out_ref, *tile_refs):
    count = points_ref.shape[0]
    for tile, tile_ref in enumerate(tile_refs[:-1]):
        tile_ref[...] = points_ref[:, tile * 128 : (tile + 1) * 128]
    tile_refs[-1][...] = jnp.concatenate(
        [
            points_ref[:, (len(tile_refs) - 1) * 128 :],
            jnp.broadcast_to(cell_ref[...], (count, KW - K)),
        ],
        axis=1,
    )
    sublane = lax.broadcasted_iota(jnp.int32, (8, 128), 0)

    def place(step, carry):
        tiles = [jnp.zeros((8, 128), jnp.float32)] * (KW // 128)
        for lane in range(8):
            source = source_ref[step * 8 + lane]
            chosen = sublane == jnp.where(source >= 0, lane, 8)
            point = jnp.maximum(source, 0)
            for tile, tile_ref in enumerate(tile_refs):
                row = tile_ref[pl.ds(point, 8, stride=0), :]
                tiles[tile] = jnp.where(chosen, row, tiles[tile])
        start = pl.multiple_of(step * 8, 8)
        for tile in range(KW // 128):
            out_ref[pl.ds(start, 8), pl.ds(tile * 128, 128)] = tiles[tile]
        return carry

    lax.fori_loop(0, out_ref.shape[0] // 8, place, 0)


def pack(source, points, cell, slots):
    return pl.pallas_call(
        pack_kernel,
        out_shape=jax.ShapeDtypeStruct((slots, KW), jnp.float32),
        in_specs=[
            pl.BlockSpec(memory_space=pltpu.SMEM),
            pl.BlockSpec(memory_space=pltpu.VMEM),
            pl.BlockSpec(memory_space=pltpu.VMEM),
        ],
        out_specs=pl.BlockSpec(memory_space=pltpu.VMEM),
        scratch_shapes=[pltpu.VMEM((points.shape[0], 128), jnp.float32)] * (KW // 128),
        compiler_params=pltpu.CompilerParams(vmem_limit_bytes=24 << 20),
        name="pack_points",
    )(source, points, cell)


def rim_forcing(outer_spectra, dest_cell, rows_dev, cols_dev):
    row_count = lax.axis_size("rows")
    col_count = lax.axis_size("cols")
    devices = row_count * col_count
    total_cols = cols_dev * col_count
    total_rows = rows_dev * row_count
    grid_row = dest_cell // total_cols
    grid_col = dest_cell % total_cols
    owner = grid_row // rows_dev * col_count + grid_col // cols_dev
    on_row = (grid_row == 0) | (grid_row == total_rows - 1)
    rim = jnp.where(on_row, grid_col % cols_dev, cols_dev + grid_row % rows_dev)
    position = jnp.arange(dest_cell.shape[0], dtype=jnp.int32)
    hot = owner[:, None] == jnp.arange(devices, dtype=jnp.int32)[None]
    before = (position[:, None] > position[None, :]).astype(jnp.bfloat16)
    earlier = jnp.dot(before, hot.astype(jnp.bfloat16), preferred_element_type=jnp.float32)
    rank = jnp.sum(jnp.where(hot, earlier, 0.0), axis=1).astype(jnp.int32)
    in_slot = rank[:, None] == jnp.arange(CAP, dtype=jnp.int32)[None]
    number = jnp.where(in_slot, (position + 1).astype(jnp.float32)[:, None], 0.0)
    source = lax.dot_general(
        hot.astype(jnp.float32),
        number,
        (((0,), (0,)), ((), ())),
        precision=lax.Precision.HIGHEST,
        preferred_element_type=jnp.float32,
    )
    source = source.astype(jnp.int32).reshape(-1) - 1
    outgoing = pack(source, outer_spectra, rim.astype(jnp.float32)[:, None], devices * CAP)
    arrived = lax.all_to_all(
        outgoing.reshape(devices, CAP, KW),
        ("rows", "cols"),
        split_axis=0,
        concat_axis=0,
        tiled=True,
    ).reshape(devices * CAP, KW)
    cells = arrived[:, K].astype(jnp.int32)
    rim_size = cols_dev + rows_dev
    member = (cells[:, None] == jnp.arange(rim_size, dtype=jnp.int32)[None]).astype(jnp.float32)
    return lax.dot_general(
        member,
        arrived[:, :K],
        (((0,), (0,)), ((), ())),
        precision=lax.Precision.HIGHEST,
        preferred_element_type=jnp.float32,
    )


def sweep_kernel(
    order_ref,
    wind_ref,
    speed_ref,
    loss_ref,
    rim_ref,
    side_ref,
    mask_ref,
    trig_ref,
    high_ref,
    low_ref,
    out_ref,
    state_ref,
    part_ref,
    total_ref,
    turned_ref,
    sem,
):
    total_ref[...] = jnp.zeros_like(total_ref)
    part_ref[...] = jnp.zeros_like(part_ref)

    def wide(x):
        return jnp.concatenate([x, x], axis=1)

    def one_sweep(iteration, turn):
        quad = order_ref[iteration, turn]
        up_x = (quad == 0) | (quad == 3)
        up_y = quad < 2
        cos_row = trig_ref[quad, 0:1, :]
        sin_row = trig_ref[quad, 1:2, :]
        both = cos_row + sin_row

        def row_of(s):
            return jnp.where(up_x, s, ROWS - 1 - s)

        def factors(s):
            row = row_of(s)
            speed = speed_ref[row]
            energy = total_ref[row] * (1.0 / K)
            damp = whitecap_rate * energy / (1.0 + energy)
            den = both * speed + loss_ref[row] + wide(damp)
            inv = 1.0 / den
            known = wind_ref[quad, row] + mask_ref[...] * side_ref[quad, row]
            if s == 0 or s == ROWS - 1:
                known = known + rim_ref[quad, jnp.where(row == 0, 0, 1)]
            if iteration > 0:
                old = state_ref[quad, row]
                beside = jnp.where(up_y, pltpu.roll(old, 1, 0), pltpu.roll(old, CW - 1, 0))
                known = known + sin_row * speed * beside
            return (cos_row * speed) * inv, known * inv

        copies = []
        nxt = factors(0)
        upwind = None
        for s in range(ROWS):
            along, fixed = nxt
            balance = fixed if s == 0 else along * upwind + fixed
            first = balance.astype(jnp.bfloat16)
            second = (balance - first.astype(jnp.float32)).astype(jnp.bfloat16)
            high = high_ref[quad]
            new = (
                jnp.dot(first, high, preferred_element_type=jnp.float32)
                + jnp.dot(second, high, preferred_element_type=jnp.float32)
                + jnp.dot(first, low_ref[quad], preferred_element_type=jnp.float32)
            )
            if s + 1 < ROWS:
                nxt = factors(s + 1)
            row = row_of(s)
            if iteration == 0:
                state_ref[quad, row] = new
            square = jnp.sum(new * new, axis=1, keepdims=True)
            square = jnp.broadcast_to(square, (CW, 128))
            total = (
                part_ref[(quad + 1) % 4, row]
                + part_ref[(quad + 2) % 4, row]
                + part_ref[(quad + 3) % 4, row]
                + square
            )
            part_ref[quad, row] = square
            total_ref[row] = total
            if iteration == ITERS - 1:
                own = new[:HALF]
                turned_ref[s] = jnp.concatenate([own, own], axis=0).T[:KQ]
                copy = pltpu.make_async_copy(
                    turned_ref.at[s],
                    out_ref.at[pl.ds(quad * KQ, KQ), row],
                    sem.at[s],
                )
                copy.start()
                copies.append(copy)
            upwind = new
        for copy in copies:
            copy.wait()

    for iteration in range(ITERS):

        def turn_body(turn, carry, iteration=iteration):
            one_sweep(iteration, turn)
            return carry

        lax.fori_loop(0, 4, turn_body, 0)


def run_sweeps(order, wind, speed, loss, rim, side, mask, trig, high, low):
    vmem = pl.BlockSpec(memory_space=pltpu.VMEM)
    return pl.pallas_call(
        sweep_kernel,
        out_shape=jax.ShapeDtypeStruct((K, ROWS, 128), jnp.float32),
        in_specs=[pl.BlockSpec(memory_space=pltpu.SMEM)] + [vmem] * 9,
        out_specs=pl.BlockSpec(memory_space=pl.ANY),
        scratch_shapes=[
            pltpu.VMEM((4, ROWS, CW, KP), jnp.float32),
            pltpu.VMEM((4, ROWS, CW, 128), jnp.float32),
            pltpu.VMEM((ROWS, CW, 128), jnp.float32),
            pltpu.VMEM((ROWS, KQ, 128), jnp.float32),
            pltpu.SemaphoreType.DMA((ROWS,)),
        ],
        compiler_params=pltpu.CompilerParams(vmem_limit_bytes=48 << 20),
        name="eight_sweeps",
    )(order, wind, speed, loss, rim, side, mask, trig, high, low)


def pad_quads(x, fill=0.0):
    parts = jnp.stack([x[..., q * KQ : (q + 1) * KQ] for q in range(4)], axis=0)
    pads = [(0, 0)] * (parts.ndim - 1) + [(0, KP - KQ)]
    return jnp.pad(parts, pads, constant_values=fill)


def with_halo(own, left, right):
    gap = jnp.zeros(own.shape[:-2] + (CW - HALF - 2, own.shape[-1]), own.dtype)
    return jnp.concatenate([own, right, gap, left], axis=-2)


def body(
    wind_speed,
    wind_dir,
    depth_class,
    group_speed,
    dissipation,
    input_rate,
    outer_spectra,
    dest_cell,
    refraction_inverse,
    sweep_order,
):
    rows_dev, cols_dev = wind_speed.shape
    col_count = lax.axis_size("cols")
    core = lax.axis_index("rows")
    chip = lax.axis_index("cols")
    swap = [(0, 1), (1, 0)]
    ahead = [(i, i + 1) for i in range(col_count - 1)]
    back = [(i + 1, i) for i in range(col_count - 1)]

    fields = jnp.stack([wind_speed, wind_dir, depth_class.astype(jnp.float32)], axis=-1)
    both = lax.all_gather(fields, "rows", axis=0, tiled=True)
    from_left = lax.ppermute(both[:, cols_dev - 1 :], "cols", ahead)
    from_right = lax.ppermute(both[:, :1], "cols", back)
    own = lax.dynamic_slice_in_dim(both, core * HALF, HALF, 1)
    left = jnp.where(core == 0, from_left, both[:, HALF - 1 : HALF])
    right = jnp.where(core == 0, both[:, HALF : HALF + 1], from_right)
    cells = with_halo(own, left, right)
    speed_in, dir_in, class_in = cells[..., 0:1], cells[..., 1:2], cells[..., 2:3]

    angle = (np.arange(NDIR, dtype=np.float64) + 0.5) * (2.0 * math.pi / NDIR)
    angle_k = np.repeat(angle, NFREQ).reshape(4, KQ)
    lanes = ((0, 0), (0, KP - KQ))
    cos_k = jnp.asarray(np.pad(np.cos(angle_k), lanes).astype(np.float32))
    sin_k = jnp.asarray(np.pad(np.sin(angle_k), lanes).astype(np.float32))
    trig = jnp.stack([jnp.abs(cos_k), jnp.abs(sin_k)], axis=1)
    rate_k = jnp.pad(jnp.tile(input_rate, QUARTER), (0, KP - KQ))
    strength = (speed_in * 0.1) ** 2
    spread = jnp.maximum(
        cos_k[:, None, None] * jnp.cos(dir_in)[None] + sin_k[:, None, None] * jnp.sin(dir_in)[None],
        0.0,
    )
    wind = (rate_k * strength)[None] * (spread * spread)

    def by_class(table, fill):
        wide = jnp.pad(
            jnp.tile(table, (1, QUARTER)), ((0, 0), (0, KP - KQ)), constant_values=fill
        )
        result = wide[0]
        for index in range(1, table.shape[0]):
            result = jnp.where(class_in == index, wide[index], result)
        return jnp.broadcast_to(result, (ROWS, CW, KP))

    speeds = by_class(group_speed, 0.0)
    losses = by_class(dissipation, 1.0)
    matrix = jnp.pad(
        jnp.swapaxes(refraction_inverse, 1, 2), ((0, 0), (0, KP - KQ), (0, KP - KQ))
    )
    rounded = lax.reduce_precision(matrix, 8, 7)
    high = rounded.astype(jnp.bfloat16)
    low = (matrix - rounded).astype(jnp.bfloat16)

    rim = rim_forcing(outer_spectra, dest_cell, rows_dev, cols_dev)
    near = lax.dynamic_slice_in_dim(rim, core * HALF, HALF, 0)
    edge = jnp.where(core == 0, rim[HALF : HALF + 1], rim[HALF - 1 : HALF])
    far = lax.dynamic_slice_in_dim(rim, (1 - core) * HALF, HALF, 0)
    far_edge = jnp.where(core == 0, rim[HALF - 1 : HALF], rim[HALF : HALF + 1])
    side = rim[cols_dev:]
    got = lax.ppermute(jnp.concatenate([far, side, far_edge], axis=0), "rows", swap)
    first, last = rim[:1], rim[cols_dev - 1 : cols_dev]

    def flat(row, col):
        return row * col_count + col

    straight = [(flat(0, c), flat(0, c + 1)) for c in range(col_count - 1)]
    straight += [(flat(1, c), flat(1, c - 1)) for c in range(1, col_count)]
    across = [(flat(1, c), flat(0, c + 1)) for c in range(col_count - 1)]
    across += [(flat(0, c), flat(1, c - 1)) for c in range(1, col_count)]
    mine_out = lax.ppermute(jnp.where(core == 0, last, first), ("rows", "cols"), straight)
    other_out = lax.ppermute(jnp.where(core == 0, first, last), ("rows", "cols"), across)

    def rim_row(inner, outer, columns):
        lefts = jnp.where(core == 0, outer, inner)
        rights = jnp.where(core == 0, inner, outer)
        return with_halo(columns, lefts, rights)

    mine = rim_row(edge, mine_out, near)
    other = rim_row(got[HALF + rows_dev :], other_out, got[:HALF])
    top = jnp.where(core == 0, mine, other)
    bottom = jnp.where(core == 0, other, mine)
    rim_rows = pad_quads(jnp.stack([top, bottom], axis=0))
    other_side = got[HALF : HALF + rows_dev]
    sides = jnp.where(
        core == 0,
        jnp.concatenate([side, other_side], axis=0),
        jnp.concatenate([other_side, side], axis=0),
    )
    side_rows = pad_quads(sides[:, None, :])
    at_col = jnp.where(
        (chip == 0) & (core == 0),
        0,
        jnp.where((chip == col_count - 1) & (core == 1), HALF - 1, CW),
    )
    mask = (jnp.arange(CW, dtype=jnp.int32) == at_col).astype(jnp.float32)
    mask = jnp.broadcast_to(mask[:, None], (CW, KP))

    out = run_sweeps(
        sweep_order, wind, speeds, losses, rim_rows, side_rows, mask, trig, high, low
    )
    keep = lax.dynamic_slice_in_dim(out, core * rows_dev, rows_dev, 1)
    give = lax.dynamic_slice_in_dim(out, (1 - core) * rows_dev, rows_dev, 1)
    taken = lax.ppermute(give, "rows", swap)
    lane_core = jnp.arange(cols_dev, dtype=jnp.int32) // HALF
    return jnp.where(lane_core == core, keep, taken)


def solution(mesh):
    placed = (
        P("rows", "cols"),
        P("rows", "cols"),
        P("rows", "cols"),
        P(),
        P(),
        P(),
        P(("rows", "cols"), None),
        P(("rows", "cols")),
        P(),
        P(),
    )
    return jax.shard_map(
        body, mesh=mesh, in_specs=placed, out_specs=P(None, "rows", "cols"), check_vma=False
    )
```

profile of v0, /device:TPU:33, one launch (start us, length us, event | category | flops | bytes accessed | tf_op | source)
XLA Modules:
  0.0 205.6 jit_solution(10271285215927336552)
XLA Ops:
  0.0 0.7 fusion.29
  0.7 0.6 fusion.4
  1.3 0.8 fusion.5
  2.2 0.1 copy.20
  2.3 0.1 sub.38.source_ref
  2.4 0.2 copy.22.cell_ref
  2.6 5.0 %copy.21.points_ref = f32[1024,864]{1,0:T(8,128)} copy(f32[1024,864]{0,1:T(8,128)} %param.18) | data formatting | bytes 7077888 | tf_op args[6]
  7.6 2.0 copy-done.1
  9.6 12.2 %pack_points.1 = f32[2048,896]{1,0:T(8,128)S(1)} custom-call(s32[2048]{0:T(1024)S(1)} %sub.38.source_ref, f32[1024,864]{1,0:T(8,128)S(1)} %copy-done.1, f32[1024,1]{1,0:T(8,128)S(1)} %copy.22.cell_ref), custom_call_target="tpu_custom_call" | custom-call | tf_op jit(solution)/shard_map/pack_points/pallas_call | solution.py:59
  21.8 3.0 %copy-done = f32[2048,896]{1,0:T(8,128)} copy-done((f32[2048,896]{1,0:T(8,128)}, f32[2048,896]{1,0:T(8,128)S(1)}, u32[]{:S(2)}) %copy-start) | copy-done | bytes 7340056
  24.9 10.9 %all-to-all-start = ((f32[128,16,896]{2,1,0:T(8,128)}), f32[128,16,896]{2,1,0:T(8,128)}, u32[]{:S(2)}, u32[]{:S(2)}) async-start(f32[128,16,896]{2,1,0:T(8,128)} %bitcast.56), calls=%async_computation | async-start | bytes 14680064 | tf_op jit(solution)/shard_map/all_to_all | solution.py:101
  35.9 1.9 all_gather.3
  37.8 0.1 fusion.43
  37.8 6.4 %collective-permute-start = (f32[16,1,3]{1,0,2:T(8,128)S(1)}, f32[16,1,3]{1,0,2:T(8,128)S(1)}, u32[]{:S(2)}, u32[]{:S(2)}) collective-permute-start(f32[16,1,3]{1,0,2:T(8,128)S(1)} %get-tuple-element.33), channel_id=1, source_target_pairs={{1,0},{2,1},{3,2},{4,3},{5,4},{6,5},{7,6},{8,7},{9,8},{10,9},{11,1... | collective-permute-start | bytes 584 | tf_op jit(solution)/shard_map/ppermute | solution.py:276
  44.2 1.9 collective-permute-start.1
  46.2 0.1 tile.13
  46.3 0.1 tile.30
  46.4 0.1 tile.32
  46.5 0.3 copy.23
  46.9 0.1 constant_dynamic-slice_fusion.2
  47.0 0.1 fusion.6
  47.1 0.1 pad.56.clone
  47.2 80.0 %collective-permute-done = f32[16,1,3]{1,0,2:T(8,128)S(1)} collective-permute-done((f32[16,1,3]{1,0,2:T(8,128)S(1)}, f32[16,1,3]{1,0,2:T(8,128)S(1)}, u32[]{:S(2)}, u32[]{:S(2)}) %collective-permute-start) | collective-permute-done | bytes 224 | tf_op jit(solution)/shard_map/ppermute | solution.py:276
  127.2 0.1 slice_select_fusion.1
  127.3 0.1 pad_maximum_fusion.4
  127.4 0.1 fusion.25
  127.5 0.2 broadcast_multiply_fusion
  127.7 2.7 %multiply_multiply_fusion.wind_ref = f32[4,16,72,256]{3,2,1,0:T(8,128)} fusion(f32[16,72]{1,0:T(8,128)S(1)} %get-tuple-element.29, f32[4,256]{1,0:T(4,128)S(1)} %copy-done.9, f32[16,72]{1,0:T(8,128)S(1)} %get-tuple-element.30, f32[4,256]{1,0:T(4,128)S(1)} %copy-done.8, f32[16,72,256]{2,1,0:T(8,128)S(1)} %broadcast_multiply_fusion), kind=kLoop, calls=%fused_computation.2 | loop fusion | flops 7077888 | bytes 5915648 | tf_op jit(solution)/shard_map/mul | solution.py:295
  130.4 1.9 fusion.7
  132.3 6.6 %fusion = f32[136,864]{1,0:T(8,128)S(1)} fusion(f32[2048,896]{1,0:T(8,128)} %bitcast.19, s32[2048]{0:T(1024)S(1)} %fusion.7), kind=kOutput, calls=%fused_computation | convolution fusion | flops 2888056832 | bytes 7818240 | tf_op jit(solution)/shard_map/dot_general | solution.py:111
  138.9 7.9 %collective-permute-start.2 = (f32[1,864]{1,0:T(1,128)S(1)}, f32[1,864]{1,0:T(1,128)S(1)}, u32[]{:S(2)}, u32[]{:S(2)}) collective-permute-start(f32[1,864]{1,0:T(1,128)S(1)} %broadcast_select_fusion.7), channel_id=1, source_target_pairs={{0,1},{1,2},{2,3},{3,4},{4,5},{5,6},{6,7},{7,8},{8,9},{9,10},{10,1... | collective-permute-start | bytes 10376 | tf_op jit(solution)/shard_map/ppermute | solution.py:331
  146.9 0.7 collective-permute-done.2
  147.6 2.3 %collective-permute-start.3 = (f32[73,864]{1,0:T(8,128)S(1)}, f32[73,864]{1,0:T(8,128)S(1)}, u32[]{:S(2)}, u32[]{:S(2)}) collective-permute-start(f32[73,864]{1,0:T(8,128)S(1)} %pad_maximum_fusion), channel_id=1, source_target_pairs={{0,64},{64,0},{1,65},{65,1},{2,66},{66,2},{3,67},{67,3},{4,68},{68... | collective-permute-start | bytes 756872 | tf_op jit(solution)/shard_map/ppermute | solution.py:321
  149.9 0.5 select_select_fusion
  150.5 2.1 %collective-permute-start.4 = (f32[1,864]{1,0:T(1,128)S(1)}, f32[1,864]{1,0:T(1,128)S(1)}, u32[]{:S(2)}, u32[]{:S(2)}) collective-permute-start(f32[1,864]{1,0:T(1,128)S(1)} %get-tuple-element.16), channel_id=1, source_target_pairs={{64,1},{65,2},{66,3},{67,4},{68,5},{69,6},{70,7},{71,8},{72,9},{73... | collective-permute-start | bytes 10376 | tf_op jit(solution)/shard_map/ppermute | solution.py:332
  152.7 0.1 broadcast_select_fusion
  152.7 0.2 slice_bitcast_fusion.4
  152.9 2.5 %collective-permute-done.4 = f32[1,864]{1,0:T(1,128)S(1)} collective-permute-done((f32[1,864]{1,0:T(1,128)S(1)}, f32[1,864]{1,0:T(1,128)S(1)}, u32[]{:S(2)}, u32[]{:S(2)}) %collective-permute-start.4) | collective-permute-done | bytes 3488 | tf_op jit(solution)/shard_map/ppermute | solution.py:332
  155.4 0.1 fusion.16
  155.5 0.2 fusion.20
  155.7 0.1 select_maximum_fusion.3.side_ref
  155.8 0.1 select_maximum_fusion.rim_ref
  155.9 0.1 broadcast_in_dim.131.mask_ref
  156.0 31.8 %eight_sweeps.1 = f32[864,16,128]{2,1,0:T(8,128)} custom-call(s32[2,4]{1,0:T(2,128)S(1)} %copy-done.3, f32[4,16,72,256]{3,2,1,0:T(8,128)} %multiply_multiply_fusion.wind_ref, f32[16,72,256]{2,1,0:T(8,128)S(1)} %get-tuple-element.36.speed_ref, f32[16,72,256]{2,1,0:T(8,128)S(1)} %get-tuple-element.35.loss_ref, ...), custom_call_target="tpu_custom_call" | custom-call | tf_op jit(solution)/shard_map/eight_sweeps/pallas_call | solution.py:225
  187.8 2.2 %constant_dynamic-slice_fusion = f32[864,8,128]{2,1,0:T(8,128)S(1)} fusion(f32[864,16,128]{2,1,0:T(8,128)} %eight_sweeps.1, s32[]{:T(128)S(6)} %select_n.217), kind=kLoop, calls=%fused_computation.127 | loop fusion | bytes 7077892 | tf_op jit(solution)/shard_map/dynamic_slice | solution.py:363
  190.0 4.3 %collective-permute-start.5 = (f32[864,8,128]{2,1,0:T(8,128)S(1)}, f32[864,8,128]{2,1,0:T(8,128)}, u32[]{:S(2)}, u32[]{:S(2)}) collective-permute-start(f32[864,8,128]{2,1,0:T(8,128)S(1)} %constant_dynamic-slice_fusion), channel_id=1, source_target_pairs={{0,64},{64,0},{1,65},{65,1},{2,66},{66,2},{3,67},{67,3},{4,68},{68... | collective-permute-start | bytes 10616840 | tf_op jit(solution)/shard_map/ppermute | solution.py:364
  194.4 6.0 %collective-permute-done.5 = f32[864,8,128]{2,1,0:T(8,128)} collective-permute-done((f32[864,8,128]{2,1,0:T(8,128)S(1)}, f32[864,8,128]{2,1,0:T(8,128)}, u32[]{:S(2)}, u32[]{:S(2)}) %collective-permute-start.5) | collective-permute-done | bytes 3538976 | tf_op jit(solution)/shard_map/ppermute | solution.py:364
  200.3 5.2 %dynamic-slice_select_fusion = f32[864,8,128]{2,1,0:T(8,128)} fusion(f32[864,8,128]{2,1,0:T(8,128)} %collective-permute-done.5, f32[864,16,128]{2,1,0:T(8,128)} %eight_sweeps.1, s32[]{:T(128)S(6)} %select_n.216, pred[128]{0:T(512)(128)(4,1)S(1)} %fusion.41), kind=kLoop, calls=%fused_computation.5 | loop fusion | flops 884736 | bytes 10616964 | tf_op jit(solution)/shard_map/jit(_where)/select_n | solution.py:366
  (50 shorter events, 0.3 us)
Async XLA Ops:
  7.6 2.0 copy-start.1
  21.8 3.0 %copy-start = (f32[2048,896]{1,0:T(8,128)}, f32[2048,896]{1,0:T(8,128)S(1)}, u32[]{:S(2)}) copy-start(f32[2048,896]{1,0:T(8,128)S(1)} %pack_points.1) | copy-start | bytes 22020100
  24.8 11.0 %copy-start.5 = (s32[8,128]{1,0:T(8,128)S(1)}, s32[8,128]{1,0:T(8,128)}, u32[]{:S(2)}) copy-start(s32[8,128]{1,0:T(8,128)} %param.14) | copy-start | bytes 12292
  24.8 11.0 %copy-start.6 = (f32[8,128]{1,0:T(8,128)S(1)}, f32[8,128]{1,0:T(8,128)}, u32[]{:S(2)}) copy-start(f32[8,128]{1,0:T(8,128)} %param.13) | copy-start | bytes 12292
  24.8 11.1 %copy-start.7 = (f32[8,128]{1,0:T(8,128)S(1)}, f32[8,128]{1,0:T(8,128)}, u32[]{:S(2)}) copy-start(f32[8,128]{1,0:T(8,128)} %param.12) | copy-start | bytes 12292
  24.8 21.3 %copy-start.12 = (f32[24]{0:T(128)S(1)}, f32[24]{0:T(128)}, u32[]{:S(2)}) copy-start(f32[24]{0:T(128)} %param.17) | copy-start | bytes 292
  24.9 21.4 %copy-start.10 = (f32[4,24]{1,0:T(4,128)S(1)}, f32[4,24]{1,0:T(4,128)}, u32[]{:S(2)}) copy-start(f32[4,24]{1,0:T(4,128)} %param.15) | copy-start | bytes 1156
  24.9 21.5 %copy-start.11 = (f32[4,24]{1,0:T(4,128)S(1)}, f32[4,24]{1,0:T(4,128)}, u32[]{:S(2)}) copy-start(f32[4,24]{1,0:T(4,128)} %param.16) | copy-start | bytes 1156
  24.9 21.6 %copy-start.4 = (f32[4,216,216]{2,1,0:T(8,128)S(1)}, f32[4,216,216]{2,1,0:T(8,128)}, u32[]{:S(2)}) copy-start(f32[4,216,216]{2,1,0:T(8,128)} %param.20) | copy-start | bytes 2239492
  24.9 105.5 %all-to-all-start = ((f32[128,16,896]{2,1,0:T(8,128)}), f32[128,16,896]{2,1,0:T(8,128)}, u32[]{:S(2)}, u32[]{:S(2)}) async-start(f32[128,16,896]{2,1,0:T(8,128)} %bitcast.56), calls=%async_computation | async-start | bytes 14680064 | tf_op jit(solution)/shard_map/all_to_all | solution.py:101
  35.8 91.8 %copy-start.8 = (f32[4,256]{1,0:T(4,128)S(1)}, f32[4,256]{1,0:T(4,128)}, u32[]{:S(2)}) copy-start(f32[4,256]{1,0:T(4,128)} %constant.128.clone) | copy-start | bytes 12292
  35.9 91.8 %copy-start.9 = (f32[4,256]{1,0:T(4,128)S(1)}, f32[4,256]{1,0:T(4,128)}, u32[]{:S(2)}) copy-start(f32[4,256]{1,0:T(4,128)} %constant.129.clone) | copy-start | bytes 12292
  37.8 89.4 %collective-permute-start = (f32[16,1,3]{1,0,2:T(8,128)S(1)}, f32[16,1,3]{1,0,2:T(8,128)S(1)}, u32[]{:S(2)}, u32[]{:S(2)}) collective-permute-start(f32[16,1,3]{1,0,2:T(8,128)S(1)} %get-tuple-element.33), channel_id=1, source_target_pairs={{1,0},{2,1},{3,2},{4,3},{5,4},{6,5},{7,6},{8,7},{9,8},{10,9},{11,1... | collective-permute-start | bytes 584 | tf_op jit(solution)/shard_map/ppermute | solution.py:276
  44.2 83.0 %collective-permute-start.1 = (f32[16,1,3]{1,0,2:T(8,128)S(1)}, f32[16,1,3]{1,0,2:T(8,128)S(1)}, u32[]{:S(2)}, u32[]{:S(2)}) collective-permute-start(f32[16,1,3]{1,0,2:T(8,128)S(1)} %get-tuple-element.34), channel_id=1, source_target_pairs={{0,1},{1,2},{2,3},{3,4},{4,5},{5,6},{6,7},{7,8},{8,9},{9,10},{10,1... | collective-permute-start | bytes 584 | tf_op jit(solution)/shard_map/ppermute | solution.py:275
  138.9 8.6 %collective-permute-start.2 = (f32[1,864]{1,0:T(1,128)S(1)}, f32[1,864]{1,0:T(1,128)S(1)}, u32[]{:S(2)}, u32[]{:S(2)}) collective-permute-start(f32[1,864]{1,0:T(1,128)S(1)} %broadcast_select_fusion.7), channel_id=1, source_target_pairs={{0,1},{1,2},{2,3},{3,4},{4,5},{5,6},{6,7},{7,8},{8,9},{9,10},{10,1... | collective-permute-start | bytes 10376 | tf_op jit(solution)/shard_map/ppermute | solution.py:331
  147.6 8.4 %copy-start.2 = (f32[4,2,256]{2,1,0:T(2,128)S(1)}, f32[4,2,256]{2,1,0:T(2,128)}, u32[]{:S(2)}) copy-start(f32[4,2,256]{2,1,0:T(2,128)} %constant.146.trig_ref) | copy-start | bytes 24580
  147.6 8.4 %copy-start.3 = (s32[2,4]{1,0:T(2,128)S(1)}, s32[2,4]{1,0:T(2,128)}, u32[]{:S(2)}) copy-start(s32[2,4]{1,0:T(2,128)} %order_ref.1) | copy-start | bytes 100
  147.6 5.0 %collective-permute-start.3 = (f32[73,864]{1,0:T(8,128)S(1)}, f32[73,864]{1,0:T(8,128)S(1)}, u32[]{:S(2)}, u32[]{:S(2)}) collective-permute-start(f32[73,864]{1,0:T(8,128)S(1)} %pad_maximum_fusion), channel_id=1, source_target_pairs={{0,64},{64,0},{1,65},{65,1},{2,66},{66,2},{3,67},{67,3},{4,68},{68... | collective-permute-start | bytes 756872 | tf_op jit(solution)/shard_map/ppermute | solution.py:321
  150.5 4.9 %collective-permute-start.4 = (f32[1,864]{1,0:T(1,128)S(1)}, f32[1,864]{1,0:T(1,128)S(1)}, u32[]{:S(2)}, u32[]{:S(2)}) collective-permute-start(f32[1,864]{1,0:T(1,128)S(1)} %get-tuple-element.16), channel_id=1, source_target_pairs={{64,1},{65,2},{66,3},{67,4},{68,5},{69,6},{70,7},{71,8},{72,9},{73... | collective-permute-start | bytes 10376 | tf_op jit(solution)/shard_map/ppermute | solution.py:332
  190.0 10.3 %collective-permute-start.5 = (f32[864,8,128]{2,1,0:T(8,128)S(1)}, f32[864,8,128]{2,1,0:T(8,128)}, u32[]{:S(2)}, u32[]{:S(2)}) collective-permute-start(f32[864,8,128]{2,1,0:T(8,128)S(1)} %constant_dynamic-slice_fusion), channel_id=1, source_target_pairs={{0,64},{64,0},{1,65},{65,1},{2,66},{66,2},{3,67},{67,3},{4,68},{68... | collective-permute-start | bytes 10616840 | tf_op jit(solution)/shard_map/ppermute | solution.py:364
where the time goes:
time: 206 us
  waiting for transfers between devices  89.2 us (43%)
  Pallas kernels  44 us (21%)
  starting transfers between devices  35.9 us (17%)
  local copies, waits for them, and re-layouts  13.9 us (7%)
  other arithmetic  12.2 us (6%)
  matrix products  8.09 us (4%)
    ppermute x1, waiting for transfers between devices, body(): from_right = lax.ppermute(both[:, :1], 'cols', back)  80 us
    pallas_call x1, Pallas kernels, run_sweeps(): pl.pallas_call(sweep_kernel, out_shape=jax.ShapeDtypeStruct((K, ROWS, 128...  31.8 us
    pallas_call x1, Pallas kernels, pack(): pl.pallas_call(pack_kernel, out_shape=jax.ShapeDtypeStruct((slots, KW), j...  12.2 us
    all_to_all x1, starting transfers between devices, rim_forcing(): lax.all_to_all(outgoing.reshape(devices, CAP, KW), ('rows', 'cols'), spli...  10.9 us
    unnamed x28, local copies, waits for them, and re-layouts  10.4 us
    ppermute x1, starting transfers between devices, body(): lax.ppermute(jnp.where(core == 0, last, first), ('rows', 'cols'), straight)  7.88 us
    dot_general x1, matrix products, rim_forcing(): lax.dot_general(member, arrived[:, :K], (((0,), (0,)), ((), ())), precisi...  6.62 us
    ppermute x1, starting transfers between devices, body(): from_right = lax.ppermute(both[:, :1], 'cols', back)  6.38 us
  transfers between devices with their start and end apart: 7, of which 4 were waited for; matrix products, arithmetic and copies ran while one was open for 2% of the time, Pallas kernels for 0%

commit v1 on v0

--- a/solution.py
+++ b/solution.py
@@ -17,7 +17,9 @@
 KQ = QUARTER * NFREQ
 KP = 256
 K = 4 * KQ
-KW = 896
+TILES = 7
+WIDE = 124
+CELLS = 144
 ROWS = 16
 HALF = 64
 CW = 72
@@ -25,50 +27,317 @@
 whitecap_rate = 0.5
 
 
-def pack_kernel(source_ref, points_ref, cell_ref, out_ref, *tile_refs):
+def place_of(order, dest):
+    at = (dest % 4, dest // 4 % 4, dest // 16)
+    return at[order] * 16 + at[(order + 1) % 3] * 4 + at[(order + 2) % 3]
+
+
+def pack_kernel(source_ref, points_ref, cell_ref, out_ref, load_ref, done_ref, *rest):
+    tile_refs, (load_sem, done_sem) = rest[:TILES], rest[TILES:]
     count = points_ref.shape[0]
-    for tile, tile_ref in enumerate(tile_refs[:-1]):
-        tile_ref[...] = points_ref[:, tile * 128 : (tile + 1) * 128]
-    tile_refs[-1][...] = jnp.concatenate(
-        [
-            points_ref[:, (len(tile_refs) - 1) * 128 :],
-            jnp.broadcast_to(cell_ref[...], (count, KW - K)),
-        ],
-        axis=1,
-    )
+    part = count // 4
+    loads = []
+    for step in range(4):
+        rows = pl.ds(step * part, part)
+        load = pltpu.make_async_copy(points_ref.at[rows], load_ref.at[rows], load_sem.at[step])
+        load.start()
+        loads.append(load)
+    for step in range(4):
+        loads[step].wait()
+        rows = pl.ds(step * part, part)
+        ids = jnp.broadcast_to(cell_ref[rows], (part, 128 - WIDE))
+        for tile, tile_ref in enumerate(tile_refs):
+            low = tile * WIDE
+            high = min(low + WIDE, K)
+            pieces = [load_ref[rows, low:high]]
+            if high - low < WIDE:
+                pieces.append(jnp.zeros((part, WIDE - high + low), jnp.float32))
+            tile_ref[rows] = jnp.concatenate(pieces + [ids], axis=1)
     sublane = lax.broadcasted_iota(jnp.int32, (8, 128), 0)
-
-    def place(step, carry):
-        tiles = [jnp.zeros((8, 128), jnp.float32)] * (KW // 128)
-        for lane in range(8):
-            source = source_ref[step * 8 + lane]
-            chosen = sublane == jnp.where(source >= 0, lane, 8)
-            point = jnp.maximum(source, 0)
-            for tile, tile_ref in enumerate(tile_refs):
-                row = tile_ref[pl.ds(point, 8, stride=0), :]
-                tiles[tile] = jnp.where(chosen, row, tiles[tile])
-        start = pl.multiple_of(step * 8, 8)
-        for tile in range(KW // 128):
-            out_ref[pl.ds(start, 8), pl.ds(tile * 128, 128)] = tiles[tile]
-        return carry
-
-    lax.fori_loop(0, out_ref.shape[0] // 8, place, 0)
-
-
-def pack(source, points, cell, slots):
+    saves = []
+    for row in range(2):
+
+        def place(step, carry, row=row):
+            tiles = [jnp.zeros((8, 128), jnp.float32)] * TILES
+            for lane in range(8):
+                source = source_ref[row * 1024 + step * 8 + lane]
+                chosen = sublane == jnp.where(source >= 0, lane, 8)
+                point = jnp.maximum(source, 0)
+                for tile, tile_ref in enumerate(tile_refs):
+                    found = tile_ref[pl.ds(point, 8, stride=0), :]
+                    tiles[tile] = jnp.where(chosen, found, tiles[tile])
+            dest = step // 2
+            half = step % 2 * 8
+            starts = [place_of(order, dest) * CAP + half for order in range(3)]
+            for tile in range(TILES):
+                start = pl.multiple_of(starts[(tile + row) % 3], 8)
+                done_ref[row, tile, pl.ds(start, 8), :] = tiles[tile]
+            return carry
+
+        lax.fori_loop(0, 128, place, 0)
+        save = pltpu.make_async_copy(done_ref.at[row], out_ref.at[row], done_sem.at[row])
+        save.start()
+        saves.append(save)
+    for save in saves:
+        save.wait()
+
+
+def pack(source, points, cell):
     return pl.pallas_call(
         pack_kernel,
-        out_shape=jax.ShapeDtypeStruct((slots, KW), jnp.float32),
+        out_shape=jax.ShapeDtypeStruct((2, TILES, 1024, 128), jnp.float32),
         in_specs=[
             pl.BlockSpec(memory_space=pltpu.SMEM),
-            pl.BlockSpec(memory_space=pltpu.VMEM),
+            pl.BlockSpec(memory_space=pl.ANY),
             pl.BlockSpec(memory_space=pltpu.VMEM),
         ],
-        out_specs=pl.BlockSpec(memory_space=pltpu.VMEM),
-        scratch_shapes=[pltpu.VMEM((points.shape[0], 128), jnp.float32)] * (KW // 128),
-        compiler_params=pltpu.CompilerParams(vmem_limit_bytes=24 << 20),
+        out_specs=pl.BlockSpec(memory_space=pl.ANY),
+        scratch_shapes=[
+            pltpu.VMEM(points.shape, jnp.float32),
+            pltpu.VMEM((2, TILES, 1024, 128), jnp.float32),
+        ]
+        + [pltpu.VMEM((points.shape[0], 128), jnp.float32)] * TILES
+        + [pltpu.SemaphoreType.DMA((4,)), pltpu.SemaphoreType.DMA((2,))],
+        compiler_params=pltpu.CompilerParams(vmem_limit_bytes=32 << 20),
         name="pack_points",
     )(source, points, cell)
+
+
+def exchange_kernel(
+    slots_ref,
+    rim_ref,
+    side_ref,
+    near_ref,
+    far_ref,
+    hot_ref,
+    dense_ref,
+    last_ref,
+    own_ref,
+    other_ref,
+    edge_ref,
+    send1,
+    recv1,
+    send2,
+    recv2,
+    send3,
+    recv3,
+    send4,
+    recv4,
+):
+    core = lax.axis_index("rows")
+    chip = lax.axis_index("cols")
+    strides = (1, 4, 16)
+    at = tuple(chip // stride % 4 for stride in strides)
+    chips = 64
+
+    def moved(axis, value):
+        return chip + (value - at[axis]) * strides[axis]
+
+    def remote(src, dst, send, recv, row, col):
+        return pltpu.make_async_remote_copy(
+            src_ref=src,
+            dst_ref=dst,
+            send_sem=send,
+            recv_sem=recv,
+            device_id=(row, col),
+            device_id_type=pl.DeviceIdType.MESH,
+        )
+
+    def drain(ref, sem):
+        pltpu.make_async_copy(ref, ref, sem).wait()
+
+    barrier = pltpu.get_barrier_semaphore()
+
+    def greet(row, col):
+        pl.semaphore_signal(
+            barrier, inc=1, device_id=(row, col), device_id_type=pl.DeviceIdType.MESH
+        )
+
+    for axis in range(3):
+        for step in range(1, 4):
+            for row in range(2):
+                greet(row, moved(axis, (at[axis] + step) % 4))
+    greet(1 - core, chip)
+
+    after, before = (chip + 1) % chips, (chip + chips - 1) % chips
+    greet(0, after)
+    greet(1, before)
+    greet(core, (chip + chips - 1 + 2 * core) % chips)
+    pl.semaphore_wait(barrier, 22)
+
+    for tile in range(TILES):
+        for row in range(2):
+            axis = (tile + row) % 3
+            mine = core * 4 + at[axis]
+            for step in range(1, 4):
+                goal = (at[axis] + step) % 4
+                remote(
+                    slots_ref.at[row, tile, pl.ds(pl.multiple_of(goal * 256, 256), 256)],
+                    near_ref.at[tile, mine],
+                    send1.at[tile],
+                    recv1.at[tile],
+                    row,
+                    moved(axis, goal),
+                ).start()
+            rest = slots_ref.at[row, tile, pl.ds(pl.multiple_of(at[axis] * 256, 256), 256)]
+
+            @pl.when(core != row)
+            def _():
+                remote(
+                    rest, near_ref.at[tile, mine], send1.at[tile], recv1.at[tile], row, chip
+                ).start()
+
+            @pl.when(core == row)
+            def _():
+                pltpu.make_async_copy(rest, near_ref.at[tile, mine], recv1.at[tile]).start()
+
+    def axis_of(tile, turn):
+        even = (tile + turn) % 3
+        odd = (tile + 1 + turn) % 3
+        place = (1 - core) * at[even] + core * at[odd]
+        stride = (1 - core) * strides[even] + core * strides[odd]
+        return place, stride
+
+    for tile in range(TILES):
+        drain(near_ref.at[tile], recv1.at[tile])
+        place, stride = axis_of(tile, 1)
+        for step in range(1, 4):
+            goal = (place + step) % 4
+            remote(
+                near_ref.at[tile, :, pl.ds(pl.multiple_of(goal * 64, 64), 64)],
+                far_ref.at[tile, place],
+                send2.at[tile],
+                recv2.at[tile],
+                core,
+                chip + (goal - place) * stride,
+            ).start()
+        pltpu.make_async_copy(
+            near_ref.at[tile, :, pl.ds(pl.multiple_of(place * 64, 64), 64)],
+            far_ref.at[tile, place],
+            recv2.at[tile],
+        ).start()
+
+    cell = lax.broadcasted_iota(jnp.int32, (CELLS, 512), 0)
+    for tile in range(TILES):
+        drain(far_ref.at[tile], recv2.at[tile])
+        for goal in range(4):
+            slab = far_ref[tile, :, :, goal * CAP : (goal + 1) * CAP, :].reshape(512, 128)
+            if tile < 3:
+                ids = slab.T[127:128, :].astype(jnp.int32)
+                hot_ref[tile, goal] = jnp.where(cell == ids, 1.0, 0.0).astype(jnp.bfloat16)
+            member = hot_ref[tile % 3, goal]
+            first = slab.astype(jnp.bfloat16)
+            second = (slab - first.astype(jnp.float32)).astype(jnp.bfloat16)
+            dense_ref[tile, goal] = jnp.dot(
+                member, first, preferred_element_type=jnp.float32
+            ) + jnp.dot(member, second, preferred_element_type=jnp.float32)
+        place, stride = axis_of(tile, 2)
+        for step in range(1, 4):
+            goal = (place + step) % 4
+            remote(
+                dense_ref.at[tile, goal],
+                last_ref.at[tile, place],
+                send3.at[tile],
+                recv3.at[tile],
+                core,
+                chip + (goal - place) * stride,
+            ).start()
+        pltpu.make_async_copy(
+            dense_ref.at[tile, place], last_ref.at[tile, place], recv3.at[tile]
+        ).start()
+    for tile in range(TILES):
+        drain(last_ref.at[tile], recv3.at[tile])
+        own_ref[tile] = (
+            last_ref[tile, 0] + last_ref[tile, 1] + last_ref[tile, 2] + last_ref[tile, 3]
+        )
+
+    swap = remote(own_ref, other_ref, send4.at[0], recv4.at[0], 1 - core, chip)
+    swap.start()
+    right = remote(
+        own_ref.at[:, pl.ds(120, 8)], edge_ref.at[core], send4.at[1], recv4.at[1 + core], 0, after
+    )
+    right.start()
+    left = remote(
+        own_ref.at[:, pl.ds(0, 8)], edge_ref.at[core], send4.at[2], recv4.at[1 + core], 1, before
+    )
+    left.start()
+    swap.wait()
+    for row in range(2):
+        drain(edge_ref.at[row], recv4.at[1 + row])
+    right.wait_send()
+    left.wait_send()
+    outside = jnp.where(core == 0, chip == 0, chip == chips - 1)
+    inside = jnp.where(outside, 0.0, 1.0)
+
+    def quads(tiles):
+        full = jnp.concatenate([part[:, :WIDE] for part in tiles], axis=1)
+        gap = jnp.zeros((full.shape[0], KP - KQ), jnp.float32)
+        return [
+            jnp.concatenate([full[:, q * KQ : (q + 1) * KQ], gap], axis=1) for q in range(4)
+        ]
+
+    gap = jnp.zeros((6, 128), jnp.float32)
+    mine = pl.ds(pl.multiple_of(core * HALF, HALF), HALF)
+    for row in range(2):
+        tiles = []
+        sides = []
+        for tile in range(TILES):
+            own, other = own_ref[tile, mine, :], other_ref[tile, mine, :]
+            columns = jnp.where(core == row, own, other)
+            low = jnp.where(core == row, own_ref[tile, 56:72, :], other_ref[tile, 56:72, :])
+            edge = edge_ref[row, tile] * inside
+            rights = jnp.where(core == 0, low[8:9], edge[0:1])
+            lefts = jnp.where(core == 0, edge[7:8], low[7:8])
+            tiles.append(jnp.concatenate([columns, rights, gap, lefts], axis=0))
+            sides.append(
+                jnp.where(core == row, own_ref[tile, 128:136, :], other_ref[tile, 128:136, :])
+            )
+        for quad, value in enumerate(quads(tiles)):
+            rim_ref[quad, row] = value
+        for quad, value in enumerate(quads(sides)):
+            for index in range(8):
+                side_ref[quad, row * 8 + index] = value[index : index + 1]
+
+    for tile in range(TILES):
+        drain(near_ref.at[tile, pl.ds(0, 7)], send1.at[tile])
+        drain(far_ref.at[tile, pl.ds(0, 3)], send2.at[tile])
+        drain(last_ref.at[tile, pl.ds(0, 3)], send3.at[tile])
+
+
+def exchange(slots):
+    dma = pltpu.SemaphoreType.DMA
+    vmem = pl.BlockSpec(memory_space=pltpu.VMEM)
+    return pl.pallas_call(
+        exchange_kernel,
+        out_shape=(
+            jax.ShapeDtypeStruct((4, 2, CW, KP), jnp.float32),
+            jax.ShapeDtypeStruct((4, ROWS, 1, KP), jnp.float32),
+        ),
+        in_specs=[pl.BlockSpec(memory_space=pl.ANY)],
+        out_specs=(vmem, vmem),
+        scratch_shapes=[
+            pltpu.VMEM((TILES, 8, 256, 128), jnp.float32),
+            pltpu.VMEM((TILES, 4, 8, 64, 128), jnp.float32),
+            pltpu.VMEM((3, 4, CELLS, 512), jnp.bfloat16),
+            pltpu.VMEM((TILES, 4, CELLS, 128), jnp.float32),
+            pltpu.VMEM((TILES, 4, CELLS, 128), jnp.float32),
+            pltpu.VMEM((TILES, CELLS, 128), jnp.float32),
+            pltpu.VMEM((TILES, CELLS, 128), jnp.float32),
+            pltpu.VMEM((2, TILES, 8, 128), jnp.float32),
+            dma((TILES,)),
+            dma((TILES,)),
+            dma((TILES,)),
+            dma((TILES,)),
+            dma((TILES,)),
+            dma((TILES,)),
+            dma((3,)),
+            dma((3,)),
+        ],
+        compiler_params=pltpu.CompilerParams(
+            vmem_limit_bytes=40 << 20, collective_id=0, has_side_effects=True
+        ),
+        name="exchange_points",
+    )(slots)
 
 
 def rim_forcing(outer_spectra, dest_cell, rows_dev, cols_dev):
@@ -97,24 +366,8 @@
         preferred_element_type=jnp.float32,
     )
     source = source.astype(jnp.int32).reshape(-1) - 1
-    outgoing = pack(source, outer_spectra, rim.astype(jnp.float32)[:, None], devices * CAP)
-    arrived = lax.all_to_all(
-        outgoing.reshape(devices, CAP, KW),
-        ("rows", "cols"),
-        split_axis=0,
-        concat_axis=0,
-        tiled=True,
-    ).reshape(devices * CAP, KW)
-    cells = arrived[:, K].astype(jnp.int32)
-    rim_size = cols_dev + rows_dev
-    member = (cells[:, None] == jnp.arange(rim_size, dtype=jnp.int32)[None]).astype(jnp.float32)
-    return lax.dot_general(
-        member,
-        arrived[:, :K],
-        (((0,), (0,)), ((), ())),
-        precision=lax.Precision.HIGHEST,
-        preferred_element_type=jnp.float32,
-    )
+    slots = pack(source, outer_spectra, rim.astype(jnp.float32)[:, None])
+    return exchange(slots)
 
 
 def sweep_kernel(
@@ -239,12 +492,6 @@
     )(order, wind, speed, loss, rim, side, mask, trig, high, low)
 
 
-def pad_quads(x, fill=0.0):
-    parts = jnp.stack([x[..., q * KQ : (q + 1) * KQ] for q in range(4)], axis=0)
-    pads = [(0, 0)] * (parts.ndim - 1) + [(0, KP - KQ)]
-    return jnp.pad(parts, pads, constant_values=fill)
-
-
 def with_halo(own, left, right):
     gap = jnp.zeros(own.shape[:-2] + (CW - HALF - 2, own.shape[-1]), own.dtype)
     return jnp.concatenate([own, right, gap, left], axis=-2)
@@ -312,42 +559,7 @@
     high = rounded.astype(jnp.bfloat16)
     low = (matrix - rounded).astype(jnp.bfloat16)
 
-    rim = rim_forcing(outer_spectra, dest_cell, rows_dev, cols_dev)
-    near = lax.dynamic_slice_in_dim(rim, core * HALF, HALF, 0)
-    edge = jnp.where(core == 0, rim[HALF : HALF + 1], rim[HALF - 1 : HALF])
-    far = lax.dynamic_slice_in_dim(rim, (1 - core) * HALF, HALF, 0)
-    far_edge = jnp.where(core == 0, rim[HALF - 1 : HALF], rim[HALF : HALF + 1])
-    side = rim[cols_dev:]
-    got = lax.ppermute(jnp.concatenate([far, side, far_edge], axis=0), "rows", swap)
-    first, last = rim[:1], rim[cols_dev - 1 : cols_dev]
-
-    def flat(row, col):
-        return row * col_count + col
-
-    straight = [(flat(0, c), flat(0, c + 1)) for c in range(col_count - 1)]
-    straight += [(flat(1, c), flat(1, c - 1)) for c in range(1, col_count)]
-    across = [(flat(1, c), flat(0, c + 1)) for c in range(col_count - 1)]
-    across += [(flat(0, c), flat(1, c - 1)) for c in range(1, col_count)]
-    mine_out = lax.ppermute(jnp.where(core == 0, last, first), ("rows", "cols"), straight)
-    other_out = lax.ppermute(jnp.where(core == 0, first, last), ("rows", "cols"), across)
-
-    def rim_row(inner, outer, columns):
-        lefts = jnp.where(core == 0, outer, inner)
-        rights = jnp.where(core == 0, inner, outer)
-        return with_halo(columns, lefts, rights)
-
-    mine = rim_row(edge, mine_out, near)
-    other = rim_row(got[HALF + rows_dev :], other_out, got[:HALF])
-    top = jnp.where(core == 0, mine, other)
-    bottom = jnp.where(core == 0, other, mine)
-    rim_rows = pad_quads(jnp.stack([top, bottom], axis=0))
-    other_side = got[HALF : HALF + rows_dev]
-    sides = jnp.where(
-        core == 0,
-        jnp.concatenate([side, other_side], axis=0),
-        jnp.concatenate([other_side, side], axis=0),
-    )
-    side_rows = pad_quads(sides[:, None, :])
+    rim_rows, side_rows = rim_forcing(outer_spectra, dest_cell, rows_dev, cols_dev)
     at_col = jnp.where(
         (chip == 0) & (core == 0),
         0,

time: 206 us -> 184 us (0.89)
  the two profiles are of different devices: /device:TPU:33 before, /device:TPU:1 now
where the time goes in v1:
time: 184 us; the launch traced here: 183 us
  Pallas kernels  134 us (73%)
  local copies, waits for them, and re-layouts  19.6 us (11%)
  other arithmetic  12.3 us (7%)
  starting transfers between devices  6.77 us (4%)
  waiting for transfers between devices  5.98 us (3%)
  blocking collectives  2.9 us (2%)
    pallas_call x1, Pallas kernels, exchange(): pl.pallas_call(exchange_kernel, out_shape=(jax.ShapeDtypeStruct((4, 2, CW...  82.4 us
    pallas_call x1, Pallas kernels, run_sweeps(): pl.pallas_call(sweep_kernel, out_shape=jax.ShapeDtypeStruct((K, ROWS, 128...  31.8 us
    pallas_call x1, Pallas kernels, pack(): pl.pallas_call(pack_kernel, out_shape=jax.ShapeDtypeStruct((2, TILES, 102...  19.5 us
    unnamed x38, local copies, waits for them, and re-layouts  6.48 us
    ppermute x1, waiting for transfers between devices, body(): taken = lax.ppermute(give, 'rows', swap)  5.97 us
    select_n x1, other arithmetic, body(): return jnp.where(lane_core == core, keep, taken)  5.24 us
    ppermute x1, starting transfers between devices, body(): from_left = lax.ppermute(both[:, cols_dev - 1:], 'cols', ahead)  4.6 us
    another operation x4, local copies, waits for them, and re-layouts, by_class(): jnp.tile(table, (1, QUARTER))  4.27 us
  transfers between devices with their start and end apart: 3, of which 1 were waited for; matrix products, arithmetic and copies ran while one was open for 9% of the time, Pallas kernels for 56%

profile of v1, /device:TPU:1, one launch (start us, length us, event | category | flops | bytes accessed | tf_op | source)
XLA Modules:
  0.0 183.2 jit_solution(13503486511994918423)
XLA Ops:
  0.0 0.8 convert_bitcast_fusion
  0.8 0.9 pad_maximum_fusion.1
  1.7 2.9 %all_gather.3 = f32[16,128,3]{1,0,2:T(8,128)S(1)} all-gather(f32[8,128,3]{1,0,2:T(8,128)S(1)} %pad_maximum_fusion.1), channel_id=1, replica_groups=mesh['rows'=2,'cols'=64] {'rows'}, dimensions={0}, use_global_device_ids=true | all-gather | bytes 36864 | tf_op jit(solution)/shard_map/all_gather | solution.py:521
  4.6 0.6 copy-done.5
  5.2 0.7 fusion.26
  5.9 1.3 collective-permute-start
  7.2 4.6 %collective-permute-start.1 = (f32[16,1,3]{1,0,2:T(8,128)}, f32[16,1,3]{1,0,2:T(8,128)}, u32[]{:S(2)}, u32[]{:S(2)}) collective-permute-start(f32[16,1,3]{1,0,2:T(8,128)} %get-tuple-element.20), channel_id=1, source_target_pairs={{0,1},{1,2},{2,3},{3,4},{4,5},{5,6},{6,7},{7,8},{8,9},{9,10},{10,1... | collective-permute-start | bytes 584 | tf_op jit(solution)/shard_map/ppermute | solution.py:522
  11.8 1.4 constant_dynamic-slice_fusion.1
  13.2 0.7 tile.12
  13.9 0.7 tile.13
  14.6 1.3 tile.31
  15.8 0.8 tile.32
  16.7 0.6 pad_slice_fusion.3
  17.3 1.3 tile.14
  18.6 0.8 tile.30
  19.4 0.6 pad_slice_fusion.7
  20.0 0.7 fusion.16
  20.7 0.6 fusion.2
  21.4 0.8 fusion.3
  22.2 0.7 copy.20
  23.0 0.9 sub.37.source_ref
  23.9 3.4 %copy.21.points_ref = f32[1024,864]{1,0:T(8,128)} copy(f32[1024,864]{0,1:T(8,128)S(1)} %copy-done.3) | data formatting | bytes 7077888 | tf_op args[6]
  27.3 0.2 copy.22.cell_ref
  27.5 2.0 %copy-done = f32[1024,864]{1,0:T(8,128)S(1)} copy-done((f32[1024,864]{1,0:T(8,128)S(1)}, f32[1024,864]{1,0:T(8,128)}, u32[]{:S(2)}) %copy-start) | copy-done | bytes 3538968
  29.5 19.5 %pack_points.1.slots_ref = f32[2,7,1024,128]{3,2,1,0:T(8,128)S(1)} custom-call(s32[2048]{0:T(1024)S(1)} %sub.37.source_ref, f32[1024,864]{1,0:T(8,128)S(1)} %copy-done, f32[1024,1]{1,0:T(8,128)S(1)} %copy.22.cell_ref), custom_call_target="tpu_custom_call" | custom-call | tf_op jit(solution)/shard_map/pack_points/pallas_call | solution.py:86
  49.0 0.0 copy-start.4
  49.1 82.4 %exchange_points.1 = (f32[4,2,72,256]{3,2,1,0:T(8,128)S(1)}, f32[4,16,1,256]{3,2,1,0:T(1,128)S(1)}) custom-call(f32[2,7,1024,128]{3,2,1,0:T(8,128)S(1)} %pack_points.1.slots_ref), custom_call_target="tpu_custom_call" | custom-call | tf_op jit(solution)/shard_map/exchange_points/pallas_call | solution.py:310
  131.5 0.0 copy-start.16
  131.5 0.0 copy-start.17
  131.6 0.3 copy.23
  131.9 0.2 fusion.4
  132.1 0.1 copy-done.15
  132.2 0.1 pad.21.clone
  132.3 0.0 collective-permute-done
  132.3 0.8 slice_select_fusion.1
  133.1 0.1 pad_maximum_fusion
  133.2 0.1 fusion.12
  133.3 0.2 broadcast_multiply_fusion
  133.6 0.0 copy-start.1
  133.6 0.0 copy-start.2
  133.6 2.7 %multiply_multiply_fusion.wind_ref = f32[4,16,72,256]{3,2,1,0:T(8,128)} fusion(f32[16,72]{1,0:T(8,128)S(1)} %get-tuple-element.15, f32[4,256]{1,0:T(4,128)S(1)} %copy-done.16, f32[16,72]{1,0:T(8,128)S(1)} %get-tuple-element.16, f32[4,256]{1,0:T(4,128)S(1)} %copy-done.17, f32[16,72,256]{2,1,0:T(8,128)S(1)} %broadcast_multiply_fusion), kind=kLoop, calls=%fused_computation | loop fusion | flops 7077888 | bytes 5915648 | tf_op jit(solution)/shard_map/mul | solution.py:542
  136.4 0.5 select_select_fusion
  136.9 0.1 broadcast_in_dim.128.mask_ref
  137.0 31.8 %eight_sweeps.1 = f32[864,16,128]{2,1,0:T(8,128)} custom-call(s32[2,4]{1,0:T(2,128)S(1)} %copy-done.2, f32[4,16,72,256]{3,2,1,0:T(8,128)} %multiply_multiply_fusion.wind_ref, f32[16,72,256]{2,1,0:T(8,128)S(1)} %get-tuple-element.22.speed_ref, f32[16,72,256]{2,1,0:T(8,128)S(1)} %get-tuple-element.21.loss_ref, f32[4,2,72,256]{3,2,1,0:T(8,128)S(1)} %get-tuple-element.7.rim_ref, ...), custom_call_target="tpu_custom_call" | custom-call | tf_op jit(solution)/shard_map/eight_sweeps/pallas_call | solution.py:478
  168.8 2.2 %constant_dynamic-slice_fusion = f32[864,8,128]{2,1,0:T(8,128)S(1)} fusion(f32[864,16,128]{2,1,0:T(8,128)} %eight_sweeps.1, s32[]{:T(128)S(6)} %select_n.118), kind=kLoop, calls=%fused_computation.78 | loop fusion | bytes 7077892 | tf_op jit(solution)/shard_map/dynamic_slice | solution.py:575
  171.1 0.9 collective-permute-start.2
  172.0 6.0 %collective-permute-done.2 = f32[864,8,128]{2,1,0:T(8,128)} collective-permute-done((f32[864,8,128]{2,1,0:T(8,128)S(1)}, f32[864,8,128]{2,1,0:T(8,128)}, u32[]{:S(2)}, u32[]{:S(2)}) %collective-permute-start.2) | collective-permute-done | bytes 3538976 | tf_op jit(solution)/shard_map/ppermute | solution.py:576
  177.9 5.2 %dynamic-slice_select_fusion = f32[864,8,128]{2,1,0:T(8,128)} fusion(f32[864,8,128]{2,1,0:T(8,128)} %collective-permute-done.2, f32[864,16,128]{2,1,0:T(8,128)} %eight_sweeps.1, s32[]{:T(128)S(6)} %select_n.117, pred[128]{0:T(512)(128)(4,1)S(1)} %fusion.24), kind=kLoop, calls=%fused_computation.3 | loop fusion | flops 884736 | bytes 10616964 | tf_op jit(solution)/shard_map/jit(_where)/select_n | solution.py:578
  (35 shorter events, 0.1 us)
Async XLA Ops:
  0.0 23.9 %copy-start.3 = (f32[1024,864]{0,1:T(8,128)S(1)}, f32[1024,864]{0,1:T(8,128)}, u32[]{:S(2)}) copy-start(f32[1024,864]{0,1:T(8,128)} %param.18) | copy-start | bytes 10616836
  4.6 0.6 copy-start.5
  5.9 126.3 %collective-permute-start = (f32[16,1,3]{1,0,2:T(8,128)}, f32[16,1,3]{1,0,2:T(8,128)}, u32[]{:S(2)}, u32[]{:S(2)}) collective-permute-start(f32[16,1,3]{1,0,2:T(8,128)} %get-tuple-element.19), channel_id=1, source_target_pairs={{1,0},{2,1},{3,2},{4,3},{5,4},{6,5},{7,6},{8,7},{9,8},{10,9},{11,1... | collective-permute-start | bytes 584 | tf_op jit(solution)/shard_map/ppermute | solution.py:523
  7.2 125.1 %collective-permute-start.1 = (f32[16,1,3]{1,0,2:T(8,128)}, f32[16,1,3]{1,0,2:T(8,128)}, u32[]{:S(2)}, u32[]{:S(2)}) collective-permute-start(f32[16,1,3]{1,0,2:T(8,128)} %get-tuple-element.20), channel_id=1, source_target_pairs={{0,1},{1,2},{2,3},{3,4},{4,5},{5,6},{6,7},{7,8},{8,9},{9,10},{10,1... | collective-permute-start | bytes 584 | tf_op jit(solution)/shard_map/ppermute | solution.py:522
  27.5 2.0 %copy-start = (f32[1024,864]{1,0:T(8,128)S(1)}, f32[1024,864]{1,0:T(8,128)}, u32[]{:S(2)}) copy-start(f32[1024,864]{1,0:T(8,128)} %copy.21.points_ref) | copy-start | bytes 10616836
  49.0 82.5 %copy-start.4 = (f32[4,216,216]{2,1,0:T(8,128)S(1)}, f32[4,216,216]{2,1,0:T(8,128)}, u32[]{:S(2)}) copy-start(f32[4,216,216]{2,1,0:T(8,128)} %param.20) | copy-start | bytes 2239492
  131.5 0.7 copy-start.15
  131.5 0.8 copy-start.6
  131.5 1.6 copy-start.7
  131.5 2.0 %copy-start.16 = (f32[4,256]{1,0:T(4,128)S(1)}, f32[4,256]{1,0:T(4,128)}, u32[]{:S(2)}) copy-start(f32[4,256]{1,0:T(4,128)} %constant.126.clone) | copy-start | bytes 12292
  131.5 2.0 %copy-start.17 = (f32[4,256]{1,0:T(4,128)S(1)}, f32[4,256]{1,0:T(4,128)}, u32[]{:S(2)}) copy-start(f32[4,256]{1,0:T(4,128)} %constant.125.clone) | copy-start | bytes 12292
  133.3 3.0 %copy-start.8 = (f32[1,256]{1,0:T(1,128)S(1)}, f32[1,256]{1,0:T(1,128)}, u32[]{:S(2)}) copy-start(f32[1,256]{1,0:T(1,128)} %get-tuple-element.26) | copy-start | bytes 3076
  133.3 3.0 %copy-start.9 = (f32[1,256]{1,0:T(1,128)S(1)}, f32[1,256]{1,0:T(1,128)}, u32[]{:S(2)}) copy-start(f32[1,256]{1,0:T(1,128)} %get-tuple-element.27) | copy-start | bytes 3076
  133.3 3.0 %copy-start.10 = (f32[1,256]{1,0:T(1,128)S(1)}, f32[1,256]{1,0:T(1,128)}, u32[]{:S(2)}) copy-start(f32[1,256]{1,0:T(1,128)} %get-tuple-element.28) | copy-start | bytes 3076
  133.3 3.0 %copy-start.11 = (f32[1,256]{1,0:T(1,128)S(1)}, f32[1,256]{1,0:T(1,128)}, u32[]{:S(2)}) copy-start(f32[1,256]{1,0:T(1,128)} %get-tuple-element.29) | copy-start | bytes 3076
  133.3 3.0 %copy-start.12 = (f32[1,256]{1,0:T(1,128)S(1)}, f32[1,256]{1,0:T(1,128)}, u32[]{:S(2)}) copy-start(f32[1,256]{1,0:T(1,128)} %get-tuple-element.30) | copy-start | bytes 3076
  133.3 3.0 %copy-start.13 = (f32[1,256]{1,0:T(1,128)S(1)}, f32[1,256]{1,0:T(1,128)}, u32[]{:S(2)}) copy-start(f32[1,256]{1,0:T(1,128)} %get-tuple-element.31) | copy-start | bytes 3076
  133.3 3.0 %copy-start.14 = (f32[1,256]{1,0:T(1,128)S(1)}, f32[1,256]{1,0:T(1,128)}, u32[]{:S(2)}) copy-start(f32[1,256]{1,0:T(1,128)} %get-tuple-element.32) | copy-start | bytes 3076
  133.6 3.4 %copy-start.1 = (f32[4,2,256]{2,1,0:T(2,128)S(1)}, f32[4,2,256]{2,1,0:T(2,128)}, u32[]{:S(2)}) copy-start(f32[4,2,256]{2,1,0:T(2,128)} %constant.139.trig_ref) | copy-start | bytes 24580
  133.6 3.4 %copy-start.2 = (s32[2,4]{1,0:T(2,128)S(1)}, s32[2,4]{1,0:T(2,128)}, u32[]{:S(2)}) copy-start(s32[2,4]{1,0:T(2,128)} %order_ref.1) | copy-start | bytes 100
  171.1 6.9 %collective-permute-start.2 = (f32[864,8,128]{2,1,0:T(8,128)S(1)}, f32[864,8,128]{2,1,0:T(8,128)}, u32[]{:S(2)}, u32[]{:S(2)}) collective-permute-start(f32[864,8,128]{2,1,0:T(8,128)S(1)} %constant_dynamic-slice_fusion), channel_id=1, source_target_pairs={{0,64},{64,0},{1,65},{65,1},{2,66},{66,2},{3,67},{67,3},{4,68},{68... | collective-permute-start | bytes 10616840 | tf_op jit(solution)/shard_map/ppermute | solution.py:576

commit v2 on v1

--- a/solution.py
+++ b/solution.py
@@ -32,81 +32,19 @@
     return at[order] * 16 + at[(order + 1) % 3] * 4 + at[(order + 2) % 3]
 
 
-def pack_kernel(source_ref, points_ref, cell_ref, out_ref, load_ref, done_ref, *rest):
-    tile_refs, (load_sem, done_sem) = rest[:TILES], rest[TILES:]
-    count = points_ref.shape[0]
-    part = count // 4
-    loads = []
-    for step in range(4):
-        rows = pl.ds(step * part, part)
-        load = pltpu.make_async_copy(points_ref.at[rows], load_ref.at[rows], load_sem.at[step])
-        load.start()
-        loads.append(load)
-    for step in range(4):
-        loads[step].wait()
-        rows = pl.ds(step * part, part)
-        ids = jnp.broadcast_to(cell_ref[rows], (part, 128 - WIDE))
-        for tile, tile_ref in enumerate(tile_refs):
-            low = tile * WIDE
-            high = min(low + WIDE, K)
-            pieces = [load_ref[rows, low:high]]
-            if high - low < WIDE:
-                pieces.append(jnp.zeros((part, WIDE - high + low), jnp.float32))
-            tile_ref[rows] = jnp.concatenate(pieces + [ids], axis=1)
-    sublane = lax.broadcasted_iota(jnp.int32, (8, 128), 0)
-    saves = []
-    for row in range(2):
-
-        def place(step, carry, row=row):
-            tiles = [jnp.zeros((8, 128), jnp.float32)] * TILES
-            for lane in range(8):
-                source = source_ref[row * 1024 + step * 8 + lane]
-                chosen = sublane == jnp.where(source >= 0, lane, 8)
-                point = jnp.maximum(source, 0)
-                for tile, tile_ref in enumerate(tile_refs):
-                    found = tile_ref[pl.ds(point, 8, stride=0), :]
-                    tiles[tile] = jnp.where(chosen, found, tiles[tile])
-            dest = step // 2
-            half = step % 2 * 8
-            starts = [place_of(order, dest) * CAP + half for order in range(3)]
-            for tile in range(TILES):
-                start = pl.multiple_of(starts[(tile + row) % 3], 8)
-                done_ref[row, tile, pl.ds(start, 8), :] = tiles[tile]
-            return carry
-
-        lax.fori_loop(0, 128, place, 0)
-        save = pltpu.make_async_copy(done_ref.at[row], out_ref.at[row], done_sem.at[row])
-        save.start()
-        saves.append(save)
-    for save in saves:
-        save.wait()
-
-
-def pack(source, points, cell):
-    return pl.pallas_call(
-        pack_kernel,
-        out_shape=jax.ShapeDtypeStruct((2, TILES, 1024, 128), jnp.float32),
-        in_specs=[
-            pl.BlockSpec(memory_space=pltpu.SMEM),
-            pl.BlockSpec(memory_space=pl.ANY),
-            pl.BlockSpec(memory_space=pltpu.VMEM),
-        ],
-        out_specs=pl.BlockSpec(memory_space=pl.ANY),
-        scratch_shapes=[
-            pltpu.VMEM(points.shape, jnp.float32),
-            pltpu.VMEM((2, TILES, 1024, 128), jnp.float32),
-        ]
-        + [pltpu.VMEM((points.shape[0], 128), jnp.float32)] * TILES
-        + [pltpu.SemaphoreType.DMA((4,)), pltpu.SemaphoreType.DMA((2,))],
-        compiler_params=pltpu.CompilerParams(vmem_limit_bytes=32 << 20),
-        name="pack_points",
-    )(source, points, cell)
-
-
 def exchange_kernel(
-    slots_ref,
+    source_ref,
+    points_ref,
+    id_ref,
+    speed_ref,
+    dir_ref,
+    class_ref,
     rim_ref,
     side_ref,
+    cols_ref,
+    load_ref,
+    stage_ref,
+    slots_ref,
     near_ref,
     far_ref,
     hot_ref,
@@ -115,6 +53,11 @@
     own_ref,
     other_ref,
     edge_ref,
+    field_ref,
+    field_other_ref,
+    field_edge_ref,
+    turn_ref,
+    load_sem,
     send1,
     recv1,
     send2,
@@ -123,6 +66,8 @@
     recv3,
     send4,
     recv4,
+    send5,
+    recv5,
 ):
     core = lax.axis_index("rows")
     chip = lax.axis_index("cols")
@@ -146,6 +91,18 @@
     def drain(ref, sem):
         pltpu.make_async_copy(ref, ref, sem).wait()
 
+    count = points_ref.shape[0]
+    part = count // 4
+    loads = []
+    for step in range(4):
+        rows = pl.ds(step * part, part)
+        load = pltpu.make_async_copy(points_ref.at[rows], load_ref.at[rows], load_sem.at[step])
+        load.start()
+        loads.append(load)
+    field_ref[0:8] = speed_ref[...]
+    field_ref[8:16] = dir_ref[...]
+    field_ref[16:24] = class_ref[...].astype(jnp.float32)
+
     barrier = pltpu.get_barrier_semaphore()
 
     def greet(row, col):
@@ -165,31 +122,98 @@
     greet(core, (chip + chips - 1 + 2 * core) % chips)
     pl.semaphore_wait(barrier, 22)
 
-    for tile in range(TILES):
+    trades = []
+    for index, (row, col) in enumerate(((1 - core, chip), (0, after), (1, before))):
+        goal_ref = field_other_ref if index == 0 else field_edge_ref.at[core]
+        arrival = recv5.at[0] if index == 0 else recv5.at[1 + core]
+        trade = remote(field_ref, goal_ref, send5.at[index], arrival, row, col)
+        trade.start()
+        trades.append(trade)
+
+    sublane = lax.broadcasted_iota(jnp.int32, (8, 128), 0)
+    for load in loads:
+        load.wait()
+    ids = jnp.broadcast_to(id_ref[...], (count, 128 - WIDE))
+    for group in ((0,), (1, 2), (3, 4), (5, 6)):
+        for tile in group:
+            low = tile * WIDE
+            high = min(low + WIDE, K)
+            pieces = [load_ref[:, low:high]]
+            if high - low < WIDE:
+                pieces.append(jnp.zeros((count, WIDE - high + low), jnp.float32))
+            stage_ref[tile, 0:count] = jnp.concatenate(pieces + [ids], axis=1)
+            stage_ref[tile, count:] = jnp.zeros((8, 128), jnp.float32)
         for row in range(2):
-            axis = (tile + row) % 3
-            mine = core * 4 + at[axis]
-            for step in range(1, 4):
-                goal = (at[axis] + step) % 4
-                remote(
-                    slots_ref.at[row, tile, pl.ds(pl.multiple_of(goal * 256, 256), 256)],
-                    near_ref.at[tile, mine],
-                    send1.at[tile],
-                    recv1.at[tile],
-                    row,
-                    moved(axis, goal),
-                ).start()
-            rest = slots_ref.at[row, tile, pl.ds(pl.multiple_of(at[axis] * 256, 256), 256)]
-
-            @pl.when(core != row)
-            def _():
-                remote(
-                    rest, near_ref.at[tile, mine], send1.at[tile], recv1.at[tile], row, chip
-                ).start()
-
-            @pl.when(core == row)
-            def _():
-                pltpu.make_async_copy(rest, near_ref.at[tile, mine], recv1.at[tile]).start()
+
+            def place(dest, carry, row=row, group=group):
+                starts = [place_of((tile + row) % 3, dest) * CAP for tile in group]
+                for half in range(2):
+                    tiles = [None] * len(group)
+                    for lane in range(8):
+                        point = source_ref[row * 1024 + dest * CAP + half * 8 + lane]
+                        for index, tile in enumerate(group):
+                            found = stage_ref.at[tile][pl.ds(point, 8, stride=0), :]
+                            tiles[index] = (
+                                found
+                                if lane == 0
+                                else jnp.where(sublane == lane, found, tiles[index])
+                            )
+                    for index, tile in enumerate(group):
+                        start = pl.multiple_of(starts[index] + half * 8, 8)
+                        slots_ref[row, tile, pl.ds(start, 8), :] = tiles[index]
+                return carry
+
+            lax.fori_loop(0, 64, place, 0)
+        for tile in group:
+            for row in range(2):
+                axis = (tile + row) % 3
+                mine = core * 4 + at[axis]
+                for step in range(1, 4):
+                    goal = (at[axis] + step) % 4
+                    remote(
+                        slots_ref.at[row, tile, pl.ds(pl.multiple_of(goal * 256, 256), 256)],
+                        near_ref.at[tile, mine],
+                        send1.at[tile],
+                        recv1.at[tile],
+                        row,
+                        moved(axis, goal),
+                    ).start()
+                rest = slots_ref.at[row, tile, pl.ds(pl.multiple_of(at[axis] * 256, 256), 256)]
+
+                @pl.when(core != row)
+                def _():
+                    remote(
+                        rest, near_ref.at[tile, mine], send1.at[tile], recv1.at[tile], row, chip
+                    ).start()
+
+                @pl.when(core == row)
+                def _():
+                    pltpu.make_async_copy(rest, near_ref.at[tile, mine], recv1.at[tile]).start()
+
+    outside = jnp.where(core == 0, chip == 0, chip == chips - 1)
+    inside = jnp.where(outside, 0.0, 1.0)
+    for trade in trades:
+        trade.wait_send()
+    drain(field_other_ref, recv5.at[0])
+    for row in range(2):
+        drain(field_edge_ref.at[row], recv5.at[1 + row])
+    own_field, other_field = field_ref[...], field_other_ref[...]
+    pad = jnp.zeros((80, 128), jnp.float32)
+    both = [jnp.where(core == row, own_field, other_field) for row in range(2)]
+    turn_ref[...] = jnp.concatenate(both + [pad], axis=0).T
+    edges = jnp.concatenate([field_edge_ref[0], field_edge_ref[1], pad], axis=0).T * inside
+    middle = turn_ref[56:72]
+    mine = pl.ds(pl.multiple_of(core * HALF, HALF), HALF)
+    gap = jnp.zeros((6, 128), jnp.float32)
+    cols_ref[...] = jnp.concatenate(
+        [
+            turn_ref[mine],
+            jnp.where(core == 0, middle[8:9], edges[0:1]),
+            gap,
+            jnp.where(core == 0, edges[127:128], middle[7:8]),
+        ],
+        axis=0,
+    )
 
     def axis_of(tile, turn):
         even = (tile + turn) % 3
@@ -266,8 +290,6 @@
         drain(edge_ref.at[row], recv4.at[1 + row])
     right.wait_send()
     left.wait_send()
-    outside = jnp.where(core == 0, chip == 0, chip == chips - 1)
-    inside = jnp.where(outside, 0.0, 1.0)
 
     def quads(tiles):
         full = jnp.concatenate([part[:, :WIDE] for part in tiles], axis=1)
@@ -276,8 +298,6 @@
             jnp.concatenate([full[:, q * KQ : (q + 1) * KQ], gap], axis=1) for q in range(4)
         ]
 
-    gap = jnp.zeros((6, 128), jnp.float32)
-    mine = pl.ds(pl.multiple_of(core * HALF, HALF), HALF)
     for row in range(2):
         tiles = []
         sides = []
@@ -304,18 +324,30 @@
         drain(last_ref.at[tile, pl.ds(0, 3)], send3.at[tile])
 
 
-def exchange(slots):
+def exchange(source, points, ids, wind_speed, wind_dir, depth_class):
     dma = pltpu.SemaphoreType.DMA
     vmem = pl.BlockSpec(memory_space=pltpu.VMEM)
+    count = points.shape[0]
     return pl.pallas_call(
         exchange_kernel,
         out_shape=(
             jax.ShapeDtypeStruct((4, 2, CW, KP), jnp.float32),
             jax.ShapeDtypeStruct((4, ROWS, 1, KP), jnp.float32),
+            jax.ShapeDtypeStruct((CW, 128), jnp.float32),
         ),
-        in_specs=[pl.BlockSpec(memory_space=pl.ANY)],
-        out_specs=(vmem, vmem),
+        in_specs=[
+            pl.BlockSpec(memory_space=pltpu.SMEM),
+            pl.BlockSpec(memory_space=pl.ANY),
+            vmem,
+            vmem,
+            vmem,
+            vmem,
+        ],
+        out_specs=(vmem, vmem, vmem),
         scratch_shapes=[
+            pltpu.VMEM(points.shape, jnp.float32),
+            pltpu.VMEM((TILES, count + 8, 128), jnp.float32),
+            pltpu.VMEM((2, TILES, 1024, 128), jnp.float32),
             pltpu.VMEM((TILES, 8, 256, 128), jnp.float32),
             pltpu.VMEM((TILES, 4, 8, 64, 128), jnp.float32),
             pltpu.VMEM((3, 4, CELLS, 512), jnp.bfloat16),
@@ -324,6 +356,11 @@
             pltpu.VMEM((TILES, CELLS, 128), jnp.float32),
             pltpu.VMEM((TILES, CELLS, 128), jnp.float32),
             pltpu.VMEM((2, TILES, 8, 128), jnp.float32),
+            pltpu.VMEM((24, 128), jnp.float32),
+            pltpu.VMEM((24, 128), jnp.float32),
+            pltpu.VMEM((2, 24, 128), jnp.float32),
+            pltpu.VMEM((128, 128), jnp.float32),
+            dma((4,)),
             dma((TILES,)),
             dma((TILES,)),
             dma((TILES,)),
@@ -332,15 +369,17 @@
             dma((TILES,)),
             dma((3,)),
             dma((3,)),
+            dma((3,)),
+            dma((3,)),
         ],
         compiler_params=pltpu.CompilerParams(
-            vmem_limit_bytes=40 << 20, collective_id=0, has_side_effects=True
+            vmem_limit_bytes=52 << 20, collective_id=0, has_side_effects=True
         ),
         name="exchange_points",
-    )(slots)
-
-
-def rim_forcing(outer_spectra, dest_cell, rows_dev, cols_dev):
+    )(source, points, ids, wind_speed, wind_dir, depth_class)
+
+
+def slot_sources(dest_cell, rows_dev, cols_dev):
     row_count = lax.axis_size("rows")
     col_count = lax.axis_size("cols")
     devices = row_count * col_count
@@ -365,23 +404,28 @@
         precision=lax.Precision.HIGHEST,
         preferred_element_type=jnp.float32,
     )
-    source = source.astype(jnp.int32).reshape(-1) - 1
-    slots = pack(source, outer_spectra, rim.astype(jnp.float32)[:, None])
-    return exchange(slots)
+    source = source.astype(jnp.int32).reshape(-1)
+    source = jnp.where(source > 0, source - 1, dest_cell.shape[0])
+    return source, rim.astype(jnp.float32)[:, None]
 
 
 def sweep_kernel(
     order_ref,
+    cols_ref,
+    rim_ref,
+    side_ref,
+    mask_ref,
+    angle_ref,
+    group_ref,
+    rate_ref,
+    matrix_ref,
+    out_ref,
     wind_ref,
     speed_ref,
     loss_ref,
-    rim_ref,
-    side_ref,
-    mask_ref,
     trig_ref,
     high_ref,
     low_ref,
-    out_ref,
     state_ref,
     part_ref,
     total_ref,
@@ -390,6 +434,42 @@
 ):
     total_ref[...] = jnp.zeros_like(total_ref)
     part_ref[...] = jnp.zeros_like(part_ref)
+    trig_ref[...] = jnp.abs(angle_ref[...])
+
+    tables = jnp.concatenate([group_ref[...], rate_ref[...]], axis=0)
+    tables = jnp.concatenate(
+        [tables] * QUARTER + [jnp.ones((tables.shape[0], KP - KQ), jnp.float32)], axis=1
+    )
+    rate = tables[8:9]
+    edge = jnp.zeros((KQ, KP - KQ), jnp.float32)
+    foot = jnp.zeros((KP - KQ, KP), jnp.float32)
+    for quad in range(4):
+        full = jnp.concatenate(
+            [jnp.concatenate([matrix_ref[quad], edge], axis=1), foot], axis=0
+        ).T
+        rounded = full.astype(jnp.bfloat16)
+        high_ref[quad] = rounded
+        low_ref[quad] = (full - rounded.astype(jnp.float32)).astype(jnp.bfloat16)
+
+    cols = cols_ref[...]
+    cols_cos, cols_sin, cols_wind = jnp.cos(cols), jnp.sin(cols), (cols * 0.1) ** 2
+    for row in range(ROWS):
+        base = row // 8 * 24 + row % 8
+        strength = rate * cols_wind[:, base : base + 1]
+        toward = cols_cos[:, base + 8 : base + 9]
+        aside = cols_sin[:, base + 8 : base + 9]
+        kind = jnp.broadcast_to(cols[:, base + 16 : base + 17], (CW, KP))
+        speed, loss = tables[0:1], tables[4:5]
+        for index in range(1, 4):
+            speed = jnp.where(kind == index, tables[index : index + 1], speed)
+            loss = jnp.where(kind == index, tables[4 + index : 5 + index], loss)
+        speed_ref[row] = speed
+        loss_ref[row] = loss
+        for quad in range(4):
+            spread = jnp.maximum(
+                angle_ref[quad, 0:1] * toward + angle_ref[quad, 1:2] * aside, 0.0
+            )
+            wind_ref[quad, row] = strength * (spread * spread)
 
     def wide(x):
         return jnp.concatenate([x, x], axis=1)
@@ -473,14 +553,20 @@
         lax.fori_loop(0, 4, turn_body, 0)
 
 
-def run_sweeps(order, wind, speed, loss, rim, side, mask, trig, high, low):
+def run_sweeps(order, cols, rim, side, mask, angles, groups, rate, matrix):
     vmem = pl.BlockSpec(memory_space=pltpu.VMEM)
     return pl.pallas_call(
         sweep_kernel,
         out_shape=jax.ShapeDtypeStruct((K, ROWS, 128), jnp.float32),
-        in_specs=[pl.BlockSpec(memory_space=pltpu.SMEM)] + [vmem] * 9,
+        in_specs=[pl.BlockSpec(memory_space=pltpu.SMEM)] + [vmem] * 8,
         out_specs=pl.BlockSpec(memory_space=pl.ANY),
         scratch_shapes=[
+            pltpu.VMEM((4, ROWS, CW, KP), jnp.float32),
+            pltpu.VMEM((ROWS, CW, KP), jnp.float32),
+            pltpu.VMEM((ROWS, CW, KP), jnp.float32),
+            pltpu.VMEM((4, 2, KP), jnp.float32),
+            pltpu.VMEM((4, KP, KP), jnp.bfloat16),
+            pltpu.VMEM((4, KP, KP), jnp.bfloat16),
             pltpu.VMEM((4, ROWS, CW, KP), jnp.float32),
             pltpu.VMEM((4, ROWS, CW, 128), jnp.float32),
             pltpu.VMEM((ROWS, CW, 128), jnp.float32),
@@ -489,12 +575,7 @@
         ],
         compiler_params=pltpu.CompilerParams(vmem_limit_bytes=48 << 20),
         name="eight_sweeps",
-    )(order, wind, speed, loss, rim, side, mask, trig, high, low)
-
-
-def with_halo(own, left, right):
-    gap = jnp.zeros(own.shape[:-2] + (CW - HALF - 2, own.shape[-1]), own.dtype)
-    return jnp.concatenate([own, right, gap, left], axis=-2)
+    )(order, cols, rim, side, mask, angles, groups, rate, matrix)
 
 
 def body(
@@ -514,52 +595,15 @@
     core = lax.axis_index("rows")
     chip = lax.axis_index("cols")
     swap = [(0, 1), (1, 0)]
-    ahead = [(i, i + 1) for i in range(col_count - 1)]
-    back = [(i + 1, i) for i in range(col_count - 1)]
-
-    fields = jnp.stack([wind_speed, wind_dir, depth_class.astype(jnp.float32)], axis=-1)
-    both = lax.all_gather(fields, "rows", axis=0, tiled=True)
-    from_left = lax.ppermute(both[:, cols_dev - 1 :], "cols", ahead)
-    from_right = lax.ppermute(both[:, :1], "cols", back)
-    own = lax.dynamic_slice_in_dim(both, core * HALF, HALF, 1)
-    left = jnp.where(core == 0, from_left, both[:, HALF - 1 : HALF])
-    right = jnp.where(core == 0, both[:, HALF : HALF + 1], from_right)
-    cells = with_halo(own, left, right)
-    speed_in, dir_in, class_in = cells[..., 0:1], cells[..., 1:2], cells[..., 2:3]
-
+    source, ids = slot_sources(dest_cell, rows_dev, cols_dev)
+    rim_rows, side_rows, cols = exchange(
+        source, outer_spectra, ids, wind_speed, wind_dir, depth_class
+    )
     angle = (np.arange(NDIR, dtype=np.float64) + 0.5) * (2.0 * math.pi / NDIR)
-    angle_k = np.repeat(angle, NFREQ).reshape(4, KQ)
-    lanes = ((0, 0), (0, KP - KQ))
-    cos_k = jnp.asarray(np.pad(np.cos(angle_k), lanes).astype(np.float32))
-    sin_k = jnp.asarray(np.pad(np.sin(angle_k), lanes).astype(np.float32))
-    trig = jnp.stack([jnp.abs(cos_k), jnp.abs(sin_k)], axis=1)
-    rate_k = jnp.pad(jnp.tile(input_rate, QUARTER), (0, KP - KQ))
-    strength = (speed_in * 0.1) ** 2
-    spread = jnp.maximum(
-        cos_k[:, None, None] * jnp.cos(dir_in)[None] + sin_k[:, None, None] * jnp.sin(dir_in)[None],
-        0.0,
-    )
-    wind = (rate_k * strength)[None] * (spread * spread)
-
-    def by_class(table, fill):
-        wide = jnp.pad(
-            jnp.tile(table, (1, QUARTER)), ((0, 0), (0, KP - KQ)), constant_values=fill
-        )
-        result = wide[0]
-        for index in range(1, table.shape[0]):
-            result = jnp.where(class_in == index, wide[index], result)
-        return jnp.broadcast_to(result, (ROWS, CW, KP))
-
-    speeds = by_class(group_speed, 0.0)
-    losses = by_class(dissipation, 1.0)
-    matrix = jnp.pad(
-        jnp.swapaxes(refraction_inverse, 1, 2), ((0, 0), (0, KP - KQ), (0, KP - KQ))
-    )
-    rounded = lax.reduce_precision(matrix, 8, 7)
-    high = rounded.astype(jnp.bfloat16)
-    low = (matrix - rounded).astype(jnp.bfloat16)
-
-    rim_rows, side_rows = rim_forcing(outer_spectra, dest_cell, rows_dev, cols_dev)
+    angle_k = np.repeat(angle, NFREQ).reshape(4, 1, KQ)
+    angles = np.concatenate([np.cos(angle_k), np.sin(angle_k)], axis=1)
+    angles = np.pad(angles, ((0, 0), (0, 0), (0, KP - KQ))).astype(np.float32)
+    groups = jnp.concatenate([group_speed, dissipation], axis=0)
     at_col = jnp.where(
         (chip == 0) & (core == 0),
         0,
@@ -569,7 +613,15 @@
     mask = jnp.broadcast_to(mask[:, None], (CW, KP))
 
     out = run_sweeps(
-        sweep_order, wind, speeds, losses, rim_rows, side_rows, mask, trig, high, low
+        sweep_order,
+        cols,
+        rim_rows,
+        side_rows,
+        mask,
+        jnp.asarray(angles),
+        groups,
+        input_rate[None],
+        refraction_inverse,
     )
     keep = lax.dynamic_slice_in_dim(out, core * rows_dev, rows_dev, 1)
     give = lax.dynamic_slice_in_dim(out, (1 - core) * rows_dev, rows_dev, 1)

time: 184 us -> 139 us (0.76)
  Pallas kernels: 134 us -> 116 us
  local copies, waits for them, and re-layouts: 19.6 us -> 7.76 us
  other arithmetic: 12.3 us -> 5.97 us
  starting transfers between devices: 6.77 us -> 1.82 us
  blocking collectives: 2.9 us -> 0 us
    pallas_call x1 -> x0, Pallas kernels: 19.5 us -> none  [pack(): pl.pallas_call(pack_kernel, out_shape=jax.ShapeDtypeStruct((2, TILES, 102...]
    ppermute x2 -> x0, starting transfers between devices: 5.88 us -> none  [the longest x1 4.6 us: body(): from_left = lax.ppermute(both[:, cols_dev - 1:], 'cols', ahead)]
    another operation x6 -> x0, local copies, waits for them, and re-layouts: 5.59 us -> none  [the longest x4 4.27 us: by_class(): jnp.tile(table, (1, QUARTER))]
    mul x3 -> x0, other arithmetic: 2.97 us -> none  [body(): wind = (rate_k * strength)[None] * (spread * spread)]
    all_gather x1 -> x0, blocking collectives: 2.9 us -> none  [body(): both = lax.all_gather(fields, 'rows', axis=0, tiled=True)]
    slice x3 -> x0, local copies, waits for them, and re-layouts: 1.9 us -> none  [the longest x2 1.21 us: by_class(): result = jnp.where(class_in == index, wide[index], result)]
    unnamed x38 -> x19, local copies, waits for them, and re-layouts: 6.48 us -> 5.03 us
  transfers between devices with their start and end apart: 3 -> 1, of which waited for: 1 -> 1; matrix products, arithmetic and copies ran while one was open for 9% -> 0% of each run, Pallas kernels for 56% -> 0%
where the time goes in v2:
time: 139 us
  Pallas kernels  116 us (83%)
  local copies, waits for them, and re-layouts  7.76 us (6%)
  other arithmetic  5.97 us (4%)
  waiting for transfers between devices  5.97 us (4%)
  starting transfers between devices  1.82 us (1%)
  matrix products  1.46 us (1%)
    pallas_call x1, Pallas kernels, exchange(): pl.pallas_call(exchange_kernel, out_shape=(jax.ShapeDtypeStruct((4, 2, CW...  83.9 us
    pallas_call x1, Pallas kernels, run_sweeps(): pl.pallas_call(sweep_kernel, out_shape=jax.ShapeDtypeStruct((K, ROWS, 128...  31.8 us
    ppermute x1, waiting for transfers between devices, body(): taken = lax.ppermute(give, 'rows', swap)  5.97 us
    select_n x1, other arithmetic, body(): return jnp.where(lane_core == core, keep, taken)  5.24 us
    unnamed x19, local copies, waits for them, and re-layouts  5.03 us
  transfers between devices with their start and end apart: 1, of which 1 were waited for; matrix products, arithmetic and copies ran while one was open for 0% of the time, Pallas kernels for 0%

profile of v2, /device:TPU:1, one launch (start us, length us, event | category | flops | bytes accessed | tf_op | source)
XLA Modules:
  0.0 138.9 jit_solution(12224011829695085529)
XLA Ops:
  0.0 0.7 fusion.14
  0.7 0.6 fusion.2
  1.3 0.8 add_select_fusion
  2.2 0.1 copy.17
  2.3 0.1 select_n.74.source_ref
  2.4 0.2 copy.19.id_ref
  2.6 0.0 copy-start.7
  2.6 0.0 copy-start.8
  2.6 0.0 copy-start.2
  2.7 0.0 copy-start.3
  2.7 0.0 copy-start.4
  2.7 5.0 %copy.18.points_ref = f32[1024,864]{1,0:T(8,128)} copy(f32[1024,864]{0,1:T(8,128)} %param.17) | data formatting | bytes 7077888 | tf_op args[6]
  7.7 0.0 copy-start
  7.7 0.0 copy-start.1
  7.7 0.0 copy-start.5
  7.7 0.0 copy-start.6
  7.7 0.0 copy-done.7
  7.7 0.0 copy-done.8
  7.7 0.0 copy-done.2
  7.7 0.0 copy-done.3
  7.7 0.0 copy-done.4
  7.8 83.9 %exchange_points.1 = (f32[4,2,72,256]{3,2,1,0:T(8,128)S(1)}, f32[4,16,1,256]{3,2,1,0:T(1,128)S(1)}, f32[72,128]{1,0:T(8,128)S(1)}) custom-call(s32[2048]{0:T(1024)S(1)} %select_n.74.source_ref, f32[1024,864]{1,0:T(8,128)} %copy.18.points_ref, f32[1024,1]{1,0:T(8,128)S(1)} %copy.19.id_ref, f32[8,128]{1,0:T(8,128)S(1)} %copy-done.2, f32[8,128]{1,0:T(8,128)S(1)} %copy-done.3, ...), custom_call_target="tpu_custom_call" | custom-call | tf_op jit(solution)/shard_map/exchange_points/pallas_call | solution.py:331
  91.7 0.1 broadcast_in_dim.49.mask_ref
  91.8 0.0 copy-done
  91.8 0.0 copy-done.1
  91.8 0.0 copy-done.5
  91.8 0.0 copy-done.6
  91.8 31.8 %eight_sweeps.1 = f32[864,16,128]{2,1,0:T(8,128)} custom-call(s32[2,4]{1,0:T(2,128)S(1)} %copy-done.5, f32[72,128]{1,0:T(8,128)S(1)} %get-tuple-element.8.cols_ref, f32[4,2,72,256]{3,2,1,0:T(8,128)S(1)} %get-tuple-element.9.rim_ref, f32[4,16,1,256]{3,2,1,0:T(1,128)S(1)} %get-tuple-element.10.side_ref, f32[72,256]{1,0:T(8,128)S(1)} %broadcast_in_dim.49.mask_ref, ...), custom_call_target="tpu_custom_call" | custom-call | tf_op jit(solution)/shard_map/eight_sweeps/pallas_call | solution.py:558
  123.6 2.2 %constant_dynamic-slice_fusion = f32[864,8,128]{2,1,0:T(8,128)S(1)} fusion(f32[864,16,128]{2,1,0:T(8,128)} %eight_sweeps.1, s32[]{:T(128)S(6)} %select_n.81), kind=kLoop, calls=%fused_computation.52 | loop fusion | bytes 7077892 | tf_op jit(solution)/shard_map/dynamic_slice | solution.py:627
  125.9 1.8 %collective-permute-start = (f32[864,8,128]{2,1,0:T(8,128)S(1)}, f32[864,8,128]{2,1,0:T(8,128)}, u32[]{:S(2)}, u32[]{:S(2)}) collective-permute-start(f32[864,8,128]{2,1,0:T(8,128)S(1)} %constant_dynamic-slice_fusion), channel_id=1, source_target_pairs={{0,64},{64,0},{1,65},{65,1},{2,66},{66,2},{3,67},{67,3},{4,68},{68... | collective-permute-start | bytes 10616840 | tf_op jit(solution)/shard_map/ppermute | solution.py:628
  127.7 6.0 %collective-permute-done = f32[864,8,128]{2,1,0:T(8,128)} collective-permute-done((f32[864,8,128]{2,1,0:T(8,128)S(1)}, f32[864,8,128]{2,1,0:T(8,128)}, u32[]{:S(2)}, u32[]{:S(2)}) %collective-permute-start) | collective-permute-done | bytes 3538976 | tf_op jit(solution)/shard_map/ppermute | solution.py:628
  133.7 5.2 %dynamic-slice_select_fusion = f32[864,8,128]{2,1,0:T(8,128)} fusion(f32[864,8,128]{2,1,0:T(8,128)} %collective-permute-done, f32[864,16,128]{2,1,0:T(8,128)} %eight_sweeps.1, s32[]{:T(128)S(6)} %select_n.80, pred[128]{0:T(512)(128)(4,1)S(1)} %fusion.22), kind=kLoop, calls=%fused_computation.2 | loop fusion | flops 884736 | bytes 10616964 | tf_op jit(solution)/shard_map/jit(_where)/select_n | solution.py:630
  (4 shorter events, 0.0 us)
Async XLA Ops:
  2.6 5.1 %copy-start.7 = (f32[4,24]{1,0:T(4,128)S(1)}, f32[4,24]{1,0:T(4,128)}, u32[]{:S(2)}) copy-start(f32[4,24]{1,0:T(4,128)} %param.15) | copy-start | bytes 1156
  2.6 5.1 %copy-start.8 = (f32[4,24]{1,0:T(4,128)S(1)}, f32[4,24]{1,0:T(4,128)}, u32[]{:S(2)}) copy-start(f32[4,24]{1,0:T(4,128)} %param.14) | copy-start | bytes 1156
  2.6 5.1 %copy-start.2 = (f32[8,128]{1,0:T(8,128)S(1)}, f32[8,128]{1,0:T(8,128)}, u32[]{:S(2)}) copy-start(f32[8,128]{1,0:T(8,128)} %speed_ref.1) | copy-start | bytes 12292
  2.7 5.1 %copy-start.3 = (f32[8,128]{1,0:T(8,128)S(1)}, f32[8,128]{1,0:T(8,128)}, u32[]{:S(2)}) copy-start(f32[8,128]{1,0:T(8,128)} %dir_ref.1) | copy-start | bytes 12292
  2.7 5.1 %copy-start.4 = (s32[8,128]{1,0:T(8,128)S(1)}, s32[8,128]{1,0:T(8,128)}, u32[]{:S(2)}) copy-start(s32[8,128]{1,0:T(8,128)} %class_ref.1) | copy-start | bytes 12292
  7.7 84.1 %copy-start = (f32[4,216,216]{2,1,0:T(8,128)S(1)}, f32[4,216,216]{2,1,0:T(8,128)}, u32[]{:S(2)}) copy-start(f32[4,216,216]{2,1,0:T(8,128)} %matrix_ref.1) | copy-start | bytes 2239492
  7.7 84.1 %copy-start.1 = (f32[4,2,256]{2,1,0:T(2,128)S(1)}, f32[4,2,256]{2,1,0:T(2,128)}, u32[]{:S(2)}) copy-start(f32[4,2,256]{2,1,0:T(2,128)} %constant.114.clone.angle_ref) | copy-start | bytes 24580
  7.7 84.1 %copy-start.5 = (s32[2,4]{1,0:T(2,128)S(1)}, s32[2,4]{1,0:T(2,128)}, u32[]{:S(2)}) copy-start(s32[2,4]{1,0:T(2,128)} %order_ref.1) | copy-start | bytes 100
  7.7 84.1 %copy-start.6 = (f32[24]{0:T(128)S(1)}, f32[24]{0:T(128)}, u32[]{:S(2)}) copy-start(f32[24]{0:T(128)} %param.16) | copy-start | bytes 292
  125.9 7.8 %collective-permute-start = (f32[864,8,128]{2,1,0:T(8,128)S(1)}, f32[864,8,128]{2,1,0:T(8,128)}, u32[]{:S(2)}, u32[]{:S(2)}) collective-permute-start(f32[864,8,128]{2,1,0:T(8,128)S(1)} %constant_dynamic-slice_fusion), channel_id=1, source_target_pairs={{0,64},{64,0},{1,65},{65,1},{2,66},{66,2},{3,67},{67,3},{4,68},{68... | collective-permute-start | bytes 10616840 | tf_op jit(solution)/shard_map/ppermute | solution.py:628

commit v3 on v2

--- a/solution.py
+++ b/solution.py
@@ -1,4 +1,3 @@
-from functools import partial
 import math
 
 import jax
@@ -91,11 +90,10 @@
     def drain(ref, sem):
         pltpu.make_async_copy(ref, ref, sem).wait()
 
-    count = points_ref.shape[0]
-    part = count // 4
+    count = points_ref.shape[1]
     loads = []
     for step in range(4):
-        rows = pl.ds(step * part, part)
+        rows = pl.ds(step * KQ, KQ)
         load = pltpu.make_async_copy(points_ref.at[rows], load_ref.at[rows], load_sem.at[step])
         load.start()
         loads.append(load)
@@ -131,17 +129,15 @@
         trades.append(trade)
 
     sublane = lax.broadcasted_iota(jnp.int32, (8, 128), 0)
-    for load in loads:
-        load.wait()
-    ids = jnp.broadcast_to(id_ref[...], (count, 128 - WIDE))
+    load_ref[K:] = jnp.zeros((load_ref.shape[0] - K, count), jnp.float32)
+    ids = jnp.broadcast_to(id_ref[...], (128 - WIDE, count))
     for group in ((0,), (1, 2), (3, 4), (5, 6)):
+        if group[0] < 2:
+            for load in loads[:1] if group[0] == 0 else loads[1:]:
+                load.wait()
         for tile in group:
-            low = tile * WIDE
-            high = min(low + WIDE, K)
-            pieces = [load_ref[:, low:high]]
-            if high - low < WIDE:
-                pieces.append(jnp.zeros((count, WIDE - high + low), jnp.float32))
-            stage_ref[tile, 0:count] = jnp.concatenate(pieces + [ids], axis=1)
+            block = load_ref[tile * WIDE : (tile + 1) * WIDE]
+            stage_ref[tile, 0:count] = jnp.concatenate([block, ids], axis=0).T
             stage_ref[tile, count:] = jnp.zeros((8, 128), jnp.float32)
         for row in range(2):
 
@@ -327,7 +323,7 @@
 def exchange(source, points, ids, wind_speed, wind_dir, depth_class):
     dma = pltpu.SemaphoreType.DMA
     vmem = pl.BlockSpec(memory_space=pltpu.VMEM)
-    count = points.shape[0]
+    count = points.shape[1]
     return pl.pallas_call(
         exchange_kernel,
         out_shape=(
@@ -345,7 +341,7 @@
         ],
         out_specs=(vmem, vmem, vmem),
         scratch_shapes=[
-            pltpu.VMEM(points.shape, jnp.float32),
+            pltpu.VMEM((K + 8, count), jnp.float32),
             pltpu.VMEM((TILES, count + 8, 128), jnp.float32),
             pltpu.VMEM((2, TILES, 1024, 128), jnp.float32),
             pltpu.VMEM((TILES, 8, 256, 128), jnp.float32),
@@ -406,7 +402,7 @@
     )
     source = source.astype(jnp.int32).reshape(-1)
     source = jnp.where(source > 0, source - 1, dest_cell.shape[0])
-    return source, rim.astype(jnp.float32)[:, None]
+    return source, rim.astype(jnp.float32)[None]
 
 
 def sweep_kernel(
@@ -419,7 +415,8 @@
     group_ref,
     rate_ref,
     matrix_ref,
-    out_ref,
+    keep_ref,
+    give_ref,
     wind_ref,
     speed_ref,
     loss_ref,
@@ -428,11 +425,13 @@
     low_ref,
     state_ref,
     part_ref,
-    total_ref,
+    damp_ref,
+    damp_next_ref,
+    final_ref,
     turned_ref,
     sem,
 ):
-    total_ref[...] = jnp.zeros_like(total_ref)
+    damp_ref[...] = jnp.zeros_like(damp_ref)
     part_ref[...] = jnp.zeros_like(part_ref)
     trig_ref[...] = jnp.abs(angle_ref[...])
 
@@ -469,12 +468,19 @@
             spread = jnp.maximum(
                 angle_ref[quad, 0:1] * toward + angle_ref[quad, 1:2] * aside, 0.0
             )
-            wind_ref[quad, row] = strength * (spread * spread)
+            source = strength * (spread * spread) + mask_ref[...] * side_ref[quad, row]
+            if row == 0:
+                source = source + rim_ref[quad, 0]
+            elif row == ROWS - 1:
+                source = source + rim_ref[quad, 1]
+            wind_ref[quad, row] = source
 
     def wide(x):
         return jnp.concatenate([x, x], axis=1)
 
-    def one_sweep(iteration, turn):
+    core = lax.axis_index("rows")
+
+    def one_sweep(iteration, turn, turn_half, damp_from, damp_to):
         quad = order_ref[iteration, turn]
         up_x = (quad == 0) | (quad == 3)
         up_y = quad < 2
@@ -488,13 +494,9 @@
         def factors(s):
             row = row_of(s)
             speed = speed_ref[row]
-            energy = total_ref[row] * (1.0 / K)
-            damp = whitecap_rate * energy / (1.0 + energy)
-            den = both * speed + loss_ref[row] + wide(damp)
+            den = both * speed + loss_ref[row] + wide(damp_from[row])
             inv = 1.0 / den
-            known = wind_ref[quad, row] + mask_ref[...] * side_ref[quad, row]
-            if s == 0 or s == ROWS - 1:
-                known = known + rim_ref[quad, jnp.where(row == 0, 0, 1)]
+            known = wind_ref[quad, row]
             if iteration > 0:
                 old = state_ref[quad, row]
                 beside = jnp.where(up_y, pltpu.roll(old, 1, 0), pltpu.roll(old, CW - 1, 0))
@@ -509,12 +511,8 @@
             balance = fixed if s == 0 else along * upwind + fixed
             first = balance.astype(jnp.bfloat16)
             second = (balance - first.astype(jnp.float32)).astype(jnp.bfloat16)
-            high = high_ref[quad]
-            new = (
-                jnp.dot(first, high, preferred_element_type=jnp.float32)
-                + jnp.dot(second, high, preferred_element_type=jnp.float32)
-                + jnp.dot(first, low_ref[quad], preferred_element_type=jnp.float32)
-            )
+            stacked = jnp.dot(jnp.concatenate([first, second], axis=0), high_ref[quad], preferred_element_type=jnp.float32)
+            new = stacked[:CW] + stacked[CW:] + jnp.dot(first, low_ref[quad], preferred_element_type=jnp.float32)
             if s + 1 < ROWS:
                 nxt = factors(s + 1)
             row = row_of(s)
@@ -529,37 +527,50 @@
                 + square
             )
             part_ref[quad, row] = square
-            total_ref[row] = total
-            if iteration == ITERS - 1:
-                own = new[:HALF]
-                turned_ref[s] = jnp.concatenate([own, own], axis=0).T[:KQ]
-                copy = pltpu.make_async_copy(
-                    turned_ref.at[s],
-                    out_ref.at[pl.ds(quad * KQ, KQ), row],
-                    sem.at[s],
+            energy = total * (1.0 / K)
+            damp_to[row] = whitecap_rate * energy / (1.0 + energy)
+            if iteration == ITERS - 1 and turn_half == 0:
+                final_ref[row] = new[:HALF]
+            if iteration == ITERS - 1 and turn_half == 1:
+                turned_ref[s] = jnp.concatenate([final_ref[row], new[:HALF]], axis=0).T[:KQ]
+                place = (pl.ds(turn // 2 * KQ, KQ), row % 8)
+
+                @pl.when(row // 8 == core)
+                def _():
+                    pltpu.make_async_copy(
+                        turned_ref.at[s], keep_ref.at[place], sem.at[s]
+                    ).start()
+
+                @pl.when(row // 8 != core)
+                def _():
+                    pltpu.make_async_copy(
+                        turned_ref.at[s], give_ref.at[place], sem.at[s]
+                    ).start()
+
+                copies.append(
+                    pltpu.make_async_copy(turned_ref.at[s], keep_ref.at[place], sem.at[s])
                 )
-                copy.start()
-                copies.append(copy)
             upwind = new
         for copy in copies:
             copy.wait()
 
     for iteration in range(ITERS):
 
-        def turn_body(turn, carry, iteration=iteration):
-            one_sweep(iteration, turn)
+        def two_turns(pair, carry, iteration=iteration):
+            one_sweep(iteration, 2 * pair, 0, damp_ref, damp_next_ref)
+            one_sweep(iteration, 2 * pair + 1, 1, damp_next_ref, damp_ref)
             return carry
 
-        lax.fori_loop(0, 4, turn_body, 0)
+        lax.fori_loop(0, 2, two_turns, 0)
 
 
 def run_sweeps(order, cols, rim, side, mask, angles, groups, rate, matrix):
     vmem = pl.BlockSpec(memory_space=pltpu.VMEM)
     return pl.pallas_call(
         sweep_kernel,
-        out_shape=jax.ShapeDtypeStruct((K, ROWS, 128), jnp.float32),
+        out_shape=(jax.ShapeDtypeStruct((2 * KQ, ROWS // 2, 128), jnp.float32),) * 2,
         in_specs=[pl.BlockSpec(memory_space=pltpu.SMEM)] + [vmem] * 8,
-        out_specs=pl.BlockSpec(memory_space=pl.ANY),
+        out_specs=(pl.BlockSpec(memory_space=pl.ANY),) * 2,
         scratch_shapes=[
             pltpu.VMEM((4, ROWS, CW, KP), jnp.float32),
             pltpu.VMEM((ROWS, CW, KP), jnp.float32),
@@ -570,12 +581,54 @@
             pltpu.VMEM((4, ROWS, CW, KP), jnp.float32),
             pltpu.VMEM((4, ROWS, CW, 128), jnp.float32),
             pltpu.VMEM((ROWS, CW, 128), jnp.float32),
+            pltpu.VMEM((ROWS, CW, 128), jnp.float32),
+            pltpu.VMEM((ROWS, HALF, KP), jnp.float32),
             pltpu.VMEM((ROWS, KQ, 128), jnp.float32),
             pltpu.SemaphoreType.DMA((ROWS,)),
         ],
         compiler_params=pltpu.CompilerParams(vmem_limit_bytes=48 << 20),
         name="eight_sweeps",
     )(order, cols, rim, side, mask, angles, groups, rate, matrix)
+
+
+def join_kernel(order_ref, keep_ref, got_ref, out_ref):
+    core = lax.axis_index("rows")
+    half = pl.program_id(2)
+    lane = lax.broadcasted_iota(jnp.int32, out_ref.shape, 2)
+    mine = lane // HALF == core
+
+    @pl.when(half == core)
+    def _():
+        out_ref[...] = jnp.where(mine, keep_ref[...], pltpu.roll(got_ref[...], HALF, 2))
+
+    @pl.when(half != core)
+    def _():
+        out_ref[...] = jnp.where(mine, pltpu.roll(keep_ref[...], HALF, 2), got_ref[...])
+
+
+def join(order, keep, got):
+    parts = 3
+    rows, lanes = keep.shape[1:]
+    block = (KQ // parts, rows, lanes)
+
+    def pair_of(pair, part, half, order_ref):
+        return (pair * parts + part, 0, 0)
+
+    def quad_of(pair, part, half, order_ref):
+        return (order_ref[ITERS - 1, pair * 2 + half] * parts + part, 0, 0)
+
+    return pl.pallas_call(
+        join_kernel,
+        out_shape=jax.ShapeDtypeStruct((K, rows, lanes), jnp.float32),
+        grid_spec=pltpu.PrefetchScalarGridSpec(
+            num_scalar_prefetch=1,
+            grid=(2, parts, 2),
+            in_specs=[pl.BlockSpec(block, pair_of), pl.BlockSpec(block, pair_of)],
+            out_specs=pl.BlockSpec(block, quad_of),
+        ),
+        compiler_params=pltpu.CompilerParams(vmem_limit_bytes=24 << 20),
+        name="join_cores",
+    )(order, keep, got)
 
 
 def body(
@@ -597,7 +650,7 @@
     swap = [(0, 1), (1, 0)]
     source, ids = slot_sources(dest_cell, rows_dev, cols_dev)
     rim_rows, side_rows, cols = exchange(
-        source, outer_spectra, ids, wind_speed, wind_dir, depth_class
+        source, outer_spectra.T, ids, wind_speed, wind_dir, depth_class
     )
     angle = (np.arange(NDIR, dtype=np.float64) + 0.5) * (2.0 * math.pi / NDIR)
     angle_k = np.repeat(angle, NFREQ).reshape(4, 1, KQ)
@@ -612,7 +665,7 @@
     mask = (jnp.arange(CW, dtype=jnp.int32) == at_col).astype(jnp.float32)
     mask = jnp.broadcast_to(mask[:, None], (CW, KP))
 
-    out = run_sweeps(
+    keep, give = run_sweeps(
         sweep_order,
         cols,
         rim_rows,
@@ -623,11 +676,7 @@
         input_rate[None],
         refraction_inverse,
     )
-    keep = lax.dynamic_slice_in_dim(out, core * rows_dev, rows_dev, 1)
-    give = lax.dynamic_slice_in_dim(out, (1 - core) * rows_dev, rows_dev, 1)
-    taken = lax.ppermute(give, "rows", swap)
-    lane_core = jnp.arange(cols_dev, dtype=jnp.int32) // HALF
-    return jnp.where(lane_core == core, keep, taken)
+    return join(sweep_order, keep, lax.ppermute(give, "rows", swap))
 
 
 def solution(mesh):

time: 139 us -> 133 us (0.957)
  Pallas kernels: 116 us -> 122 us
  local copies, waits for them, and re-layouts: 7.76 us -> 2.33 us
  other arithmetic: 5.97 us -> 1.51 us
  waiting for transfers between devices: 5.97 us -> 3.32 us
    pallas_call x1 -> x2, Pallas kernels: 31.8 us -> 37.9 us  [the longest x1 31.9 us: run_sweeps(): pl.pallas_call(sweep_kernel, out_shape=(jax.ShapeDtypeStruct((2 * KQ, ROW...]
    select_n x1 -> x0, other arithmetic: 5.24 us -> none  [body(): return jnp.where(lane_core == core, keep, taken)]
    unnamed x19 -> x14, local copies, waits for them, and re-layouts: 5.03 us -> 2.07 us
    ppermute x1, waiting for transfers between devices: 5.97 us -> 3.32 us  [body(): return join(sweep_order, keep, lax.ppermute(give, 'rows', swap))]
    dynamic_slice x1 -> x0, local copies, waits for them, and re-layouts: 2.24 us -> none  [body(): give = lax.dynamic_slice_in_dim(out, (1 - core) * rows_dev, rows_dev, 1)]
where the time goes in v3:
time: 133 us; the launch traced here: 132 us
  Pallas kernels  122 us (92%)
  waiting for transfers between devices  3.32 us (2%)
  local copies, waits for them, and re-layouts  2.33 us (2%)
  starting transfers between devices  1.82 us (1%)
  other arithmetic  1.51 us (1%)
  matrix products  1.46 us (1%)
    pallas_call x1, Pallas kernels, exchange(): pl.pallas_call(exchange_kernel, out_shape=(jax.ShapeDtypeStruct((4, 2, CW...  83.8 us
    pallas_call x1, Pallas kernels, run_sweeps(): pl.pallas_call(sweep_kernel, out_shape=(jax.ShapeDtypeStruct((2 * KQ, ROW...  31.9 us
    pallas_call x1, Pallas kernels, join(): pl.pallas_call(join_kernel, out_shape=jax.ShapeDtypeStruct((K, rows, lane...  6 us
    ppermute x1, waiting for transfers between devices, body(): return join(sweep_order, keep, lax.ppermute(give, 'rows', swap))  3.32 us
  transfers between devices with their start and end apart: 1, of which 1 were waited for; matrix products, arithmetic and copies ran while one was open for 0% of the time, Pallas kernels for 0%

profile of v3, /device:TPU:1, one launch (start us, length us, event | category | flops | bytes accessed | tf_op | source)
XLA Modules:
  0.0 132.3 jit_solution(435630514263830859)
XLA Ops:
  0.0 0.0 copy-start.1
  0.0 0.0 copy-start.5
  0.0 0.0 copy-start
  0.0 0.0 copy-start.6
  0.0 0.8 fusion.14
  0.8 0.6 fusion.2
  1.5 0.8 add_select_fusion
  2.3 0.1 copy.14
  2.4 0.1 select_n.58.source_ref
  2.5 0.7 pad_maximum_fusion.group_ref
  3.2 0.0 copy-start.2
  3.2 0.7 copy-done.2
  3.9 0.0 copy-start.3
  3.9 0.7 copy-done.3
  4.6 0.0 copy-start.4
  4.6 0.7 copy-done.4
  5.3 83.8 %exchange_points.1 = (f32[4,2,72,256]{3,2,1,0:T(8,128)S(1)}, f32[4,16,1,256]{3,2,1,0:T(1,128)S(1)}, f32[72,128]{1,0:T(8,128)S(1)}) custom-call(s32[2048]{0:T(1024)S(1)} %select_n.58.source_ref, f32[864,1024]{1,0:T(8,128)} %bitcast.5, f32[1,1024]{1,0:T(1,128)S(1)} %bitcast.3, f32[8,128]{1,0:T(8,128)S(1)} %copy-done.2, f32[8,128]{1,0:T(8,128)S(1)} %copy-done.3, ...), custom_call_target="tpu_custom_call" | custom-call | tf_op jit(solution)/shard_map/exchange_points/pallas_call | solution.py:327
  89.1 0.1 broadcast_in_dim.44.mask_ref
  89.2 0.0 copy-done.1
  89.2 0.0 copy-done.5
  89.2 0.0 copy-done
  89.2 0.0 copy-done.6
  89.3 31.9 %eight_sweeps.1 = (f32[432,8,128]{2,1,0:T(8,128)S(1)}, f32[432,8,128]{2,1,0:T(8,128)S(1)}) custom-call(s32[2,4]{1,0:T(2,128)S(1)} %copy-done.5, f32[72,128]{1,0:T(8,128)S(1)} %get-tuple-element.10.cols_ref, f32[4,2,72,256]{3,2,1,0:T(8,128)S(1)} %get-tuple-element.11.rim_ref, f32[4,16,1,256]{3,2,1,0:T(1,128)S(1)} %get-tuple-element.12.side_ref, ...), custom_call_target="tpu_custom_call" | custom-call | tf_op jit(solution)/shard_map/eight_sweeps/pallas_call | solution.py:569
  121.2 1.8 %collective-permute-start = (f32[432,8,128]{2,1,0:T(8,128)S(1)}, f32[432,8,128]{2,1,0:T(8,128)S(1)}, u32[]{:S(2)}, u32[]{:S(2)}) collective-permute-start(f32[432,8,128]{2,1,0:T(8,128)S(1)} %get-tuple-element.14), channel_id=1, source_target_pairs={{0,64},{64,0},{1,65},{65,1},{2,66},{66,2},{3,67},{67,3},{4,68},{68... | collective-permute-start | bytes 5308424 | tf_op jit(solution)/shard_map/ppermute | solution.py:679
  123.0 3.3 %collective-permute-done.got_ref = f32[432,8,128]{2,1,0:T(8,128)S(1)} collective-permute-done((f32[432,8,128]{2,1,0:T(8,128)S(1)}, f32[432,8,128]{2,1,0:T(8,128)S(1)}, u32[]{:S(2)}, u32[]{:S(2)}) %collective-permute-start) | collective-permute-done | bytes 1769504 | tf_op jit(solution)/shard_map/ppermute | solution.py:679
  126.3 6.0 %join_cores.1 = f32[864,8,128]{2,1,0:T(8,128)} custom-call(s32[2,4]{1,0:T(2,128)S(1)} %copy-done.5, f32[432,8,128]{2,1,0:T(8,128)S(1)} %get-tuple-element.13.keep_ref, f32[432,8,128]{2,1,0:T(8,128)S(1)} %collective-permute-done.got_ref), custom_call_target="tpu_custom_call" | custom-call | tf_op jit(solution)/shard_map/join_cores/pallas_call | solution.py:620
  (2 shorter events, 0.0 us)
Async XLA Ops:
  0.0 89.2 %copy-start.1 = (f32[4,2,256]{2,1,0:T(2,128)S(1)}, f32[4,2,256]{2,1,0:T(2,128)}, u32[]{:S(2)}) copy-start(f32[4,2,256]{2,1,0:T(2,128)} %constant.98.clone.angle_ref) | copy-start | bytes 24580
  0.0 89.2 %copy-start.5 = (s32[2,4]{1,0:T(2,128)S(1)}, s32[2,4]{1,0:T(2,128)}, u32[]{:S(2)}) copy-start(s32[2,4]{1,0:T(2,128)} %order_ref.3) | copy-start | bytes 100
  0.0 89.2 %copy-start = (f32[4,216,216]{2,1,0:T(8,128)S(1)}, f32[4,216,216]{2,1,0:T(8,128)}, u32[]{:S(2)}) copy-start(f32[4,216,216]{2,1,0:T(8,128)} %matrix_ref.1) | copy-start | bytes 2239492
  0.0 89.2 %copy-start.6 = (f32[24]{0:T(128)S(1)}, f32[24]{0:T(128)}, u32[]{:S(2)}) copy-start(f32[24]{0:T(128)} %param.16) | copy-start | bytes 292
  3.2 0.7 copy-start.2
  3.9 0.7 copy-start.3
  4.6 0.7 copy-start.4
  121.2 5.1 %collective-permute-start = (f32[432,8,128]{2,1,0:T(8,128)S(1)}, f32[432,8,128]{2,1,0:T(8,128)S(1)}, u32[]{:S(2)}, u32[]{:S(2)}) collective-permute-start(f32[432,8,128]{2,1,0:T(8,128)S(1)} %get-tuple-element.14), channel_id=1, source_target_pairs={{0,64},{64,0},{1,65},{65,1},{2,66},{66,2},{3,67},{67,3},{4,68},{68... | collective-permute-start | bytes 5308424 | tf_op jit(solution)/shard_map/ppermute | solution.py:679

commit v4 on v3

v4 whole, which is shorter than its diff:
```python
import math

import jax
import jax.numpy as jnp
import numpy as np
from jax import lax
from jax.experimental import pallas as pl
from jax.experimental.pallas import tpu as pltpu
from jax.sharding import PartitionSpec as P

NDIR = 36
NFREQ = 24
CAP = 16
ITERS = 2
QUARTER = NDIR // 4
KQ = QUARTER * NFREQ
KP = 256
K = 4 * KQ
TILES = 7
WIDE = 124
CELLS = 144
ROWS = 16
HALF = 64
CW = 72

whitecap_rate = 0.5


def place_of(order, dest):
    at = (dest % 4, dest // 4 % 4, dest // 16)
    return at[order] * 16 + at[(order + 1) % 3] * 4 + at[(order + 2) % 3]


def wave_kernel(
    source_ref,
    order_ref,
    points_ref,
    id_ref,
    wind_speed_ref,
    wind_dir_ref,
    class_ref,
    angle_ref,
    group_ref,
    dissipation_ref,
    rate_ref,
    matrix_ref,
    keep_ref,
    got_ref,
    load_ref,
    stage_ref,
    slots_ref,
    near_ref,
    far_ref,
    hot_ref,
    dense_ref,
    last_ref,
    own_ref,
    other_ref,
    edge_ref,
    field_ref,
    field_other_ref,
    field_edge_ref,
    turn_ref,
    wind_ref,
    speed_ref,
    loss_ref,
    trig_ref,
    high_ref,
    low_ref,
    state_ref,
    part_ref,
    damp_ref,
    damp_next_ref,
    final_ref,
    turned_ref,
    leave_ref,
    load_sem,
    send1,
    recv1,
    send2,
    recv2,
    send3,
    recv3,
    send4,
    recv4,
    send_edge,
    recv_edge,
    send5,
    recv5,
    save_sem,
    send6,
    recv6,
):
    core = lax.axis_index("rows")
    chip = lax.axis_index("cols")
    strides = (1, 4, 16)
    at = tuple(chip // stride % 4 for stride in strides)
    chips = 64

    def moved(axis, value):
        return chip + (value - at[axis]) * strides[axis]

    def remote(src, dst, send, recv, row, col):
        return pltpu.make_async_remote_copy(
            src_ref=src,
            dst_ref=dst,
            send_sem=send,
            recv_sem=recv,
            device_id=(row, col),
            device_id_type=pl.DeviceIdType.MESH,
        )

    def drain(ref, sem):
        pltpu.make_async_copy(ref, ref, sem).wait()

    count = points_ref.shape[1]
    loads = []
    for step in range(4):
        rows = pl.ds(step * KQ, KQ)
        load = pltpu.make_async_copy(points_ref.at[rows], load_ref.at[step], load_sem.at[step])
        load.start()
        loads.append(load)
    field_ref[0:8] = wind_speed_ref[...]
    field_ref[8:16] = wind_dir_ref[...]
    field_ref[16:24] = class_ref[...].astype(jnp.float32)

    barrier = pltpu.get_barrier_semaphore()

    def greet(row, col):
        pl.semaphore_signal(
            barrier, inc=1, device_id=(row, col), device_id_type=pl.DeviceIdType.MESH
        )

    for axis in range(3):
        for step in range(1, 4):
            for row in range(2):
                greet(row, moved(axis, (at[axis] + step) % 4))
    greet(1 - core, chip)

    after, before = (chip + 1) % chips, (chip + chips - 1) % chips
    greet(0, after)
    greet(1, before)
    greet(core, (chip + chips - 1 + 2 * core) % chips)
    pl.semaphore_wait(barrier, 22)

    trades = []
    for index, (row, col) in enumerate(((1 - core, chip), (0, after), (1, before))):
        goal_ref = field_other_ref if index == 0 else field_edge_ref.at[core]
        arrival = recv5.at[0] if index == 0 else recv5.at[1 + core]
        trade = remote(field_ref, goal_ref, send5.at[index], arrival, row, col)
        trade.start()
        trades.append(trade)

    sublane = lax.broadcasted_iota(jnp.int32, (8, 128), 0)
    for load in loads:
        load.wait()
    ids = jnp.broadcast_to(id_ref[...], (128 - WIDE, count))
    for group in ((0,), (1, 2), (3, 4), (5, 6)):
        for tile in group:
            pieces, low = [], tile * WIDE
            while low < min(tile * WIDE + WIDE, K):
                turn = low // KQ
                high = min(tile * WIDE + WIDE, turn * KQ + KQ)
                pieces.append(load_ref[order_ref[0, turn], low - turn * KQ : high - turn * KQ, :])
                low = high
            if low < tile * WIDE + WIDE:
                pieces.append(jnp.zeros((tile * WIDE + WIDE - low, count), jnp.float32))
            stage_ref[tile % 2, 0:count] = jnp.concatenate(pieces + [ids], axis=0).T
            stage_ref[tile % 2, count:] = jnp.zeros((8, 128), jnp.float32)
        for row in range(2):

            def place(dest, carry, row=row, group=group):
                starts = [place_of((tile + row) % 3, dest) * CAP for tile in group]
                for half in range(2):
                    tiles = [None] * len(group)
                    for lane in range(8):
                        point = source_ref[row * 1024 + dest * CAP + half * 8 + lane]
                        for index, tile in enumerate(group):
                            found = stage_ref.at[tile % 2][pl.ds(point, 8, stride=0), :]
                            tiles[index] = (
                                found
                                if lane == 0
                                else jnp.where(sublane == lane, found, tiles[index])
                            )
                    for index, tile in enumerate(group):
                        start = pl.multiple_of(starts[index] + half * 8, 8)
                        slots_ref[row, tile, pl.ds(start, 8), :] = tiles[index]
                return carry

            lax.fori_loop(0, 64, place, 0)
        for tile in group:
            for row in range(2):
                axis = (tile + row) % 3
                mine = core * 4 + at[axis]
                for step in range(1, 4):
                    goal = (at[axis] + step) % 4
                    remote(
                        slots_ref.at[row, tile, pl.ds(pl.multiple_of(goal * 256, 256), 256)],
                        near_ref.at[tile, mine],
                        send1.at[tile],
                        recv1.at[tile],
                        row,
                        moved(axis, goal),
                    ).start()
                rest = slots_ref.at[row, tile, pl.ds(pl.multiple_of(at[axis] * 256, 256), 256)]

                @pl.when(core != row)
                def _():
                    remote(
                        rest, near_ref.at[tile, mine], send1.at[tile], recv1.at[tile], row, chip
                    ).start()

                @pl.when(core == row)
                def _():
                    pltpu.make_async_copy(rest, near_ref.at[tile, mine], recv1.at[tile]).start()

    outside = jnp.where(core == 0, chip == 0, chip == chips - 1)
    inside = jnp.where(outside, 0.0, 1.0)
    for trade in trades:
        trade.wait_send()
    drain(field_other_ref, recv5.at[0])
    for row in range(2):
        drain(field_edge_ref.at[row], recv5.at[1 + row])
    own_field, other_field = field_ref[...], field_other_ref[...]
    pad = jnp.zeros((80, 128), jnp.float32)
    both = [jnp.where(core == row, own_field, other_field) for row in range(2)]
    turn_ref[...] = jnp.concatenate(both + [pad], axis=0).T
    edges = jnp.concatenate([field_edge_ref[0], field_edge_ref[1], pad], axis=0).T * inside
    middle = turn_ref[56:72]
    mine = pl.ds(pl.multiple_of(core * HALF, HALF), HALF)
    gap = jnp.zeros((6, 128), jnp.float32)
    cols = jnp.concatenate(
        [
            turn_ref[mine],
            jnp.where(core == 0, middle[8:9], edges[0:1]),
            gap,
            jnp.where(core == 0, edges[127:128], middle[7:8]),
        ],
        axis=0,
    )

    cols_cos, cols_sin, cols_wind = jnp.cos(cols), jnp.sin(cols), (cols * 0.1) ** 2

    def over_quadrant(table):
        fill = jnp.ones((table.shape[0], KP - KQ), jnp.float32)
        return jnp.concatenate([table] * QUARTER + [fill], axis=1)

    groups = over_quadrant(group_ref[...])
    losses = over_quadrant(dissipation_ref[...])
    rate = over_quadrant(rate_ref[...])

    def matrices():
        trig_ref[...] = jnp.abs(angle_ref[...])
        beside = jnp.zeros((KQ, KP - KQ), jnp.float32)
        below = jnp.zeros((KP - KQ, KP), jnp.float32)
        for quad in range(4):
            full = jnp.concatenate(
                [jnp.concatenate([matrix_ref[quad], beside], axis=1), below], axis=0
            ).T
            rounded = full.astype(jnp.bfloat16)
            high_ref[quad] = rounded
            low_ref[quad] = (full - rounded.astype(jnp.float32)).astype(jnp.bfloat16)

    def wind_rows(rows):
        for row in rows:
            base = row // 8 * 24 + row % 8
            strength = rate * cols_wind[:, base : base + 1]
            toward = cols_cos[:, base + 8 : base + 9]
            aside = cols_sin[:, base + 8 : base + 9]
            kind = jnp.broadcast_to(cols[:, base + 16 : base + 17], (CW, KP))
            speed, loss = groups[0:1], losses[0:1]
            for index in range(1, 4):
                speed = jnp.where(kind == index, groups[index : index + 1], speed)
                loss = jnp.where(kind == index, losses[index : index + 1], loss)
            speed_ref[row] = speed
            loss_ref[row] = loss
            for turn in range(4):
                quad = order_ref[0, turn]
                spread = jnp.maximum(
                    angle_ref[quad, 0:1] * toward + angle_ref[quad, 1:2] * aside, 0.0
                )
                wind_ref[turn, row] = strength * (spread * spread)

    def axis_of(tile, turn):
        even = (tile + turn) % 3
        odd = (tile + 1 + turn) % 3
        place = (1 - core) * at[even] + core * at[odd]
        stride = (1 - core) * strides[even] + core * strides[odd]
        return place, stride

    def relay(tile):
        drain(near_ref.at[tile], recv1.at[tile])
        place, stride = axis_of(tile, 1)
        for step in range(1, 4):
            goal = (place + step) % 4
            remote(
                near_ref.at[tile, :, pl.ds(pl.multiple_of(goal * 64, 64), 64)],
                far_ref.at[tile, place],
                send2.at[tile],
                recv2.at[tile],
                core,
                chip + (goal - place) * stride,
            ).start()
        pltpu.make_async_copy(
            near_ref.at[tile, :, pl.ds(pl.multiple_of(place * 64, 64), 64)],
            far_ref.at[tile, place],
            recv2.at[tile],
        ).start()

    cell = lax.broadcasted_iota(jnp.int32, (CELLS, 512), 0)

    def sums(tile):
        drain(far_ref.at[tile], recv2.at[tile])
        for goal in range(4):
            slab = far_ref[tile, :, :, goal * CAP : (goal + 1) * CAP, :].reshape(512, 128)
            if tile < 3:
                ids = slab.T[127:128, :].astype(jnp.int32)
                hot_ref[tile, goal] = jnp.where(cell == ids, 1.0, 0.0).astype(jnp.bfloat16)
            member = hot_ref[tile % 3, goal]
            first = slab.astype(jnp.bfloat16)
            second = (slab - first.astype(jnp.float32)).astype(jnp.bfloat16)
            dense_ref[tile, goal] = jnp.dot(
                member, first, preferred_element_type=jnp.float32
            ) + jnp.dot(member, second, preferred_element_type=jnp.float32)
        place, stride = axis_of(tile, 2)
        for step in range(1, 4):
            goal = (place + step) % 4
            remote(
                dense_ref.at[tile, goal],
                last_ref.at[tile, place],
                send3.at[tile],
                recv3.at[tile],
                core,
                chip + (goal - place) * stride,
            ).start()
        pltpu.make_async_copy(
            dense_ref.at[tile, place], last_ref.at[tile, place], recv3.at[tile]
        ).start()

    def spread(turn):
        first, tiles = 2 * turn, min(2, TILES - 2 * turn)
        for tile in range(first, first + tiles):
            drain(last_ref.at[tile], recv3.at[tile])
            own_ref[tile] = (
                last_ref[tile, 0] + last_ref[tile, 1] + last_ref[tile, 2] + last_ref[tile, 3]
            )
        part_of = pl.ds(first, tiles)
        copies = [
            remote(
                own_ref.at[part_of],
                other_ref.at[part_of],
                send4.at[turn],
                recv4.at[turn],
                1 - core,
                chip,
            ),
            remote(
                own_ref.at[part_of, pl.ds(120, 8)],
                edge_ref.at[core, part_of],
                send_edge.at[turn, 0],
                recv_edge.at[turn, core],
                0,
                after,
            ),
            remote(
                own_ref.at[part_of, pl.ds(0, 8)],
                edge_ref.at[core, part_of],
                send_edge.at[turn, 1],
                recv_edge.at[turn, core],
                1,
                before,
            ),
        ]
        for copy in copies:
            copy.start()
        return copies

    sublane_at = lax.broadcasted_iota(jnp.int32, (CW, KP), 0)
    left_end = jnp.where(chip == 0, 1, 0) * (1 - core)
    right_end = jnp.where(chip == chips - 1, 1, 0) * core
    at_col = 1000 - 1000 * left_end - (1000 - HALF + 1) * right_end
    on_side = jnp.where(sublane_at == at_col, 1.0, 0.0)

    def force(turn, copies):
        first, tiles = 2 * turn, min(2, TILES - 2 * turn)
        drain(other_ref.at[pl.ds(first, tiles)], recv4.at[turn])
        for row in range(2):
            drain(edge_ref.at[row, pl.ds(first, tiles)], recv_edge.at[turn, row])
        for copy in copies:
            copy.wait_send()
        low = turn * KQ
        used = range(low // WIDE, (low + KQ - 1) // WIDE + 1)
        cut = low - used[0] * WIDE

        def components(tiles):
            full = jnp.concatenate([part[:, :WIDE] for part in tiles], axis=1)
            fill = jnp.zeros((full.shape[0], KP - KQ), jnp.float32)
            return jnp.concatenate([full[:, cut : cut + KQ], fill], axis=1)

        for row in range(2):
            tiles, sides = [], []
            for tile in used:
                columns = jnp.where(core == row, own_ref[tile, mine, :], other_ref[tile, mine, :])
                low_part = jnp.where(
                    core == row, own_ref[tile, 56:72, :], other_ref[tile, 56:72, :]
                )
                edge = edge_ref[row, tile] * inside
                rights = jnp.where(core == 0, low_part[8:9], edge[0:1])
                lefts = jnp.where(core == 0, edge[7:8], low_part[7:8])
                tiles.append(jnp.concatenate([columns, rights, gap, lefts], axis=0))
                sides.append(
                    jnp.where(core == row, own_ref[tile, 128:136, :], other_ref[tile, 128:136, :])
                )
            rim, side = components(tiles), components(sides)
            for index in range(8):
                source = wind_ref[turn, row * 8 + index] + on_side * side[index : index + 1]
                if index == 7 * row:
                    source = source + rim
                wind_ref[turn, row * 8 + index] = source

    def wide(x):
        return jnp.concatenate([x, x], axis=1)

    def quad_at(iteration, turn):
        return order_ref[iteration, turn]

    def is_up(quad):
        return jnp.where((quad == 0) | (quad == 3), 1, 0)

    def prior(quad):
        place = jnp.where(quad_at(0, 3) == quad, 3, 0)
        place = jnp.where(quad_at(0, 2) == quad, 2, place)
        return jnp.where(quad_at(0, 1) == quad, 1, place)

    def one_sweep(iteration, turn, half, previous, damp_from, damp_to):
        quad = quad_at(iteration, turn)
        up = is_up(quad)
        up_y = quad < 2
        slot = turn if iteration == 0 else prior(quad)
        cos_row = trig_ref[quad, 0:1, :]
        sin_row = trig_ref[quad, 1:2, :]
        both = cos_row + sin_row

        def as_if(other_up, s):
            return jnp.where(other_up == up, s, ROWS - 1 - s)

        if iteration == 0:
            others = [(past, is_up(quad_at(0, past))) for past in range(turn)]
        else:
            others = []
            for step in range(1, 4):
                past = (turn + step) % 4
                past_quad = quad_at(1, past)
                index = jnp.where(past > turn, prior(past_quad), 4 + past)
                others.append((index, is_up(past_quad)))
        up_before = None if previous is None else is_up(previous)

        def factors(s):
            row = jnp.where(up == 1, s, ROWS - 1 - s)
            speed = speed_ref[row]
            den = both * speed + loss_ref[row]
            if previous is not None:
                den = den + wide(damp_from[as_if(up_before, s)])
            inv = 1.0 / den
            known = wind_ref[slot, row]
            if iteration > 0:
                old = state_ref[slot, s]
                beside = jnp.where(up_y, pltpu.roll(old, 1, 0), pltpu.roll(old, CW - 1, 0))
                known = known + sin_row * speed * beside
            return (cos_row * speed) * inv, known * inv

        nxt = factors(0)
        upwind = None
        for s in range(ROWS):
            along, fixed = nxt
            balance = fixed if s == 0 else along * upwind + fixed
            first = balance.astype(jnp.bfloat16)
            second = (balance - first.astype(jnp.float32)).astype(jnp.bfloat16)
            stacked = jnp.dot(
                jnp.concatenate([first, second], axis=0),
                high_ref[quad],
                preferred_element_type=jnp.float32,
            )
            new = (
                stacked[:CW]
                + stacked[CW:]
                + jnp.dot(first, low_ref[quad], preferred_element_type=jnp.float32)
            )
            if s + 1 < ROWS:
                nxt = factors(s + 1)
            if iteration == 0:
                state_ref[turn, s] = new
            square = jnp.sum(new * new, axis=1, keepdims=True)
            square = jnp.broadcast_to(square, (CW, 128))
            total = square
            for index, other_up in others:
                total = total + part_ref[index, as_if(other_up, s)]
            part_ref[4 * iteration + turn, s] = square
            energy = total * (1.0 / K)
            damp_to[s] = whitecap_rate * energy / (1.0 + energy)
            if iteration == ITERS - 1 and half == 0:
                final_ref[s] = new[:HALF]
            if iteration == ITERS - 1 and half == 1:
                pair = [final_ref[as_if(up_before, s)], new[:HALF]]
                turned_ref[s] = jnp.concatenate(pair, axis=0).T[:KQ]
            upwind = new
        return up

    trades = {}
    damps = (damp_ref, damp_next_ref)

    def first_sweep(turn):
        force(turn, trades.pop(turn))
        previous = None if turn == 0 else quad_at(0, turn - 1)
        one_sweep(0, turn, turn % 2, previous, damps[turn % 2], damps[1 - turn % 2])

    def spread_out(turn):
        trades[turn] = spread(turn)

    relay(0)
    relay(1)
    relay(2)
    matrices()
    wind_rows(range(ROWS))
    relay(3)
    relay(4)
    relay(5)
    relay(6)
    sums(0)
    sums(1)
    sums(2)
    sums(3)
    sums(4)
    sums(5)
    sums(6)
    spread_out(0)
    spread_out(1)
    first_sweep(0)
    spread_out(2)
    first_sweep(1)
    spread_out(3)
    first_sweep(2)
    first_sweep(3)

    def two_turns(pair, carry):
        earlier = jnp.where(pair == 0, quad_at(0, 3), quad_at(1, 1))
        one_sweep(1, 2 * pair, 0, earlier, damp_ref, damp_next_ref)
        between = quad_at(1, 2 * pair)
        up = one_sweep(1, 2 * pair + 1, 1, between, damp_next_ref, damp_ref)
        for row in range(ROWS):
            leave_ref[pair, row] = turned_ref[jnp.where(up == 1, row, ROWS - 1 - row)]
            owner = row // 8
            place = (pl.ds(pair * KQ, KQ), row % 8)

            @pl.when(core == owner)
            def _():
                pltpu.make_async_copy(
                    leave_ref.at[pair, row], keep_ref.at[place], save_sem.at[pair]
                ).start()

            @pl.when(core != owner)
            def _():
                remote(
                    leave_ref.at[pair, row],
                    got_ref.at[place],
                    send6.at[pair],
                    recv6.at[pair],
                    1 - core,
                    chip,
                ).start()

        return carry

    lax.fori_loop(0, 2, two_turns, 0)
    for tile in range(TILES):
        drain(near_ref.at[tile, pl.ds(0, 7)], send1.at[tile])
        drain(far_ref.at[tile, pl.ds(0, 3)], send2.at[tile])
        drain(last_ref.at[tile, pl.ds(0, 3)], send3.at[tile])
    for pair in range(2):
        block = leave_ref.at[pair, pl.ds(0, 8)]
        drain(block, save_sem.at[pair])
        drain(block, send6.at[pair])
        drain(block, recv6.at[pair])


def wave_sweeps(source, order, points, ids, fields, angles, tables, matrix):
    dma = pltpu.SemaphoreType.DMA
    vmem = pl.BlockSpec(memory_space=pltpu.VMEM)
    smem = pl.BlockSpec(memory_space=pltpu.SMEM)
    anywhere = pl.BlockSpec(memory_space=pl.ANY)
    count = points.shape[1]
    return pl.pallas_call(
        wave_kernel,
        out_shape=(jax.ShapeDtypeStruct((2 * KQ, ROWS // 2, 128), jnp.float32),) * 2,
        in_specs=[smem, smem, anywhere] + [vmem] * 9,
        out_specs=(anywhere, anywhere),
        scratch_shapes=[
            pltpu.VMEM((4, KQ, count), jnp.float32),
            pltpu.VMEM((2, count + 8, 128), jnp.float32),
            pltpu.VMEM((2, TILES, 1024, 128), jnp.float32),
            pltpu.VMEM((TILES, 8, 256, 128), jnp.float32),
            pltpu.VMEM((TILES, 4, 8, 64, 128), jnp.float32),
            pltpu.VMEM((3, 4, CELLS, 512), jnp.bfloat16),
            pltpu.VMEM((TILES, 4, CELLS, 128), jnp.float32),
            pltpu.VMEM((TILES, 4, CELLS, 128), jnp.float32),
            pltpu.VMEM((TILES, CELLS, 128), jnp.float32),
            pltpu.VMEM((TILES, CELLS, 128), jnp.float32),
            pltpu.VMEM((2, TILES, 8, 128), jnp.float32),
            pltpu.VMEM((24, 128), jnp.float32),
            pltpu.VMEM((24, 128), jnp.float32),
            pltpu.VMEM((2, 24, 128), jnp.float32),
            pltpu.VMEM((128, 128), jnp.float32),
            pltpu.VMEM((4, ROWS, CW, KP), jnp.float32),
            pltpu.VMEM((ROWS, CW, KP), jnp.float32),
            pltpu.VMEM((ROWS, CW, KP), jnp.float32),
            pltpu.VMEM((4, 2, KP), jnp.float32),
            pltpu.VMEM((4, KP, KP), jnp.bfloat16),
            pltpu.VMEM((4, KP, KP), jnp.bfloat16),
            pltpu.VMEM((4, ROWS, CW, KP), jnp.float32),
            pltpu.VMEM((8, ROWS, CW, 128), jnp.float32),
            pltpu.VMEM((ROWS, CW, 128), jnp.float32),
            pltpu.VMEM((ROWS, CW, 128), jnp.float32),
            pltpu.VMEM((ROWS, HALF, KP), jnp.float32),
            pltpu.VMEM((ROWS, KQ, 128), jnp.float32),
            pltpu.VMEM((2, ROWS, KQ, 128), jnp.float32),
            dma((4,)),
            dma((TILES,)),
            dma((TILES,)),
            dma((TILES,)),
            dma((TILES,)),
            dma((TILES,)),
            dma((TILES,)),
            dma((4,)),
            dma((4,)),
            dma((4, 2)),
            dma((4, 2)),
            dma((3,)),
            dma((3,)),
            dma((2,)),
            dma((2,)),
            dma((2,)),
        ],
        compiler_params=pltpu.CompilerParams(
            vmem_limit_bytes=60 << 20, collective_id=0, has_side_effects=True
        ),
        name="wave_sweeps",
    )(source, order, points, ids, *fields, angles, *tables, matrix)


def slot_sources(dest_cell, rows_dev, cols_dev):
    row_count = lax.axis_size("rows")
    col_count = lax.axis_size("cols")
    devices = row_count * col_count
    total_cols = cols_dev * col_count
    total_rows = rows_dev * row_count
    grid_row = dest_cell // total_cols
    grid_col = dest_cell % total_cols
    owner = grid_row // rows_dev * col_count + grid_col // cols_dev
    on_row = (grid_row == 0) | (grid_row == total_rows - 1)
    rim = jnp.where(on_row, grid_col % cols_dev, cols_dev + grid_row % rows_dev)
    position = jnp.arange(dest_cell.shape[0], dtype=jnp.int32)
    hot = owner[:, None] == jnp.arange(devices, dtype=jnp.int32)[None]
    before = (position[:, None] > position[None, :]).astype(jnp.bfloat16)
    earlier = jnp.dot(before, hot.astype(jnp.bfloat16), preferred_element_type=jnp.float32)
    rank = jnp.sum(jnp.where(hot, earlier, 0.0), axis=1).astype(jnp.int32)
    in_slot = rank[:, None] == jnp.arange(CAP, dtype=jnp.int32)[None]
    number = jnp.where(in_slot, (position + 1).astype(jnp.float32)[:, None], 0.0)
    source = lax.dot_general(
        hot.astype(jnp.float32),
        number,
        (((0,), (0,)), ((), ())),
        precision=lax.Precision.HIGHEST,
        preferred_element_type=jnp.float32,
    )
    source = source.astype(jnp.int32).reshape(-1)
    source = jnp.where(source > 0, source - 1, dest_cell.shape[0])
    return source, rim.astype(jnp.float32)[None]


def join_kernel(order_ref, keep_ref, got_ref, out_ref):
    core = lax.axis_index("rows")
    half = pl.program_id(2)
    lane = lax.broadcasted_iota(jnp.int32, out_ref.shape, 2)
    mine = lane // HALF == core

    @pl.when(half == core)
    def _():
        out_ref[...] = jnp.where(mine, keep_ref[...], pltpu.roll(got_ref[...], HALF, 2))

    @pl.when(half != core)
    def _():
        out_ref[...] = jnp.where(mine, pltpu.roll(keep_ref[...], HALF, 2), got_ref[...])


def join(order, keep, got):
    parts = 3
    rows, lanes = keep.shape[1:]
    block = (KQ // parts, rows, lanes)

    def pair_of(pair, part, half, order_ref):
        return (pair * parts + part, 0, 0)

    def quad_of(pair, part, half, order_ref):
        return (order_ref[ITERS - 1, pair * 2 + half] * parts + part, 0, 0)

    return pl.pallas_call(
        join_kernel,
        out_shape=jax.ShapeDtypeStruct((K, rows, lanes), jnp.float32),
        grid_spec=pltpu.PrefetchScalarGridSpec(
            num_scalar_prefetch=1,
            grid=(2, parts, 2),
            in_specs=[pl.BlockSpec(block, pair_of), pl.BlockSpec(block, pair_of)],
            out_specs=pl.BlockSpec(block, quad_of),
        ),
        compiler_params=pltpu.CompilerParams(vmem_limit_bytes=24 << 20),
        name="join_cores",
    )(order, keep, got)


def body(
    wind_speed,
    wind_dir,
    depth_class,
    group_speed,
    dissipation,
    input_rate,
    outer_spectra,
    dest_cell,
    refraction_inverse,
    sweep_order,
):
    rows_dev, cols_dev = wind_speed.shape
    source, ids = slot_sources(dest_cell, rows_dev, cols_dev)
    angle = (np.arange(NDIR, dtype=np.float64) + 0.5) * (2.0 * math.pi / NDIR)
    angle_k = np.repeat(angle, NFREQ).reshape(4, 1, KQ)
    angles = np.concatenate([np.cos(angle_k), np.sin(angle_k)], axis=1)
    angles = np.pad(angles, ((0, 0), (0, 0), (0, KP - KQ))).astype(np.float32)
    keep, got = wave_sweeps(
        source,
        sweep_order,
        outer_spectra.T,
        ids,
        (wind_speed, wind_dir, depth_class),
        jnp.asarray(angles),
        (group_speed, dissipation, input_rate[None]),
        refraction_inverse,
    )
    return join(sweep_order, keep, got)


def solution(mesh):
    placed = (
        P("rows", "cols"),
        P("rows", "cols"),
        P("rows", "cols"),
        P(),
        P(),
        P(),
        P(("rows", "cols"), None),
        P(("rows", "cols")),
        P(),
        P(),
    )
    return jax.shard_map(
        body, mesh=mesh, in_specs=placed, out_specs=P(None, "rows", "cols"), check_vma=False
    )
```

time: 133 us -> 121 us (0.910)
  Pallas kernels: 122 us -> 114 us
  waiting for transfers between devices: 3.32 us -> 0 us
  starting transfers between devices: 1.82 us -> 0 us
  local copies, waits for them, and re-layouts: 2.33 us -> 3.74 us
    pallas_call x2 -> x1, Pallas kernels: 116 us -> 108 us  [wave_sweeps(): pl.pallas_call(wave_kernel, out_shape=(jax.ShapeDtypeStruct((2 * KQ, ROWS...]
    ppermute x1 -> x0, waiting for transfers between devices: 3.32 us -> none  [body(): return join(sweep_order, keep, lax.ppermute(give, 'rows', swap))]
    ppermute x1 -> x0, starting transfers between devices: 1.82 us -> none  [body(): return join(sweep_order, keep, lax.ppermute(give, 'rows', swap))]
    unnamed x14 -> x6, local copies, waits for them, and re-layouts: 2.07 us -> 2.95 us
  transfers between devices with their start and end apart: 1 -> 0, of which waited for: 1 -> 0; matrix products, arithmetic and copies ran while one was open for 0% -> 0% of each run, Pallas kernels for 0% -> 0%
where the time goes in v4:
time: 121 us
  Pallas kernels  114 us (94%)
  local copies, waits for them, and re-layouts  3.74 us (3%)
  matrix products  1.46 us (1%)
  other arithmetic  1.3 us (1%)
    pallas_call x1, Pallas kernels, wave_sweeps(): pl.pallas_call(wave_kernel, out_shape=(jax.ShapeDtypeStruct((2 * KQ, ROWS...  108 us
    pallas_call x1, Pallas kernels, join(): pl.pallas_call(join_kernel, out_shape=jax.ShapeDtypeStruct((K, rows, lane...  5.99 us
    unnamed x6, local copies, waits for them, and re-layouts  2.95 us

profile of v4, /device:TPU:1, one launch (start us, length us, event | category | flops | bytes accessed | tf_op | source)
XLA Modules:
  0.0 120.8 jit_solution(14671627597475212720)
XLA Ops:
  0.0 1.3 %fusion.14 = (f32[1024]{0:T(1024)}, s32[1024]{0:T(1024)S(1)}, f32[1024]{0:T(1024)S(1)}) fusion(s32[1024]{0:T(1024)} %param.18), kind=kLoop, calls=%fused_computation.32 | loop fusion | flops 68608 | bytes 16384 | tf_op jit(solution)/shard_map/convert_element_type | solution.py:677
  1.3 0.0 copy-start.2
  1.3 0.6 fusion.2
  1.9 0.8 add_select_fusion
  2.8 0.1 copy.14
  2.9 0.7 select_n.50.source_ref
  3.6 108.3 %wave_sweeps.1 = (f32[432,8,128]{2,1,0:T(8,128)}, f32[432,8,128]{2,1,0:T(8,128)}) custom-call(s32[2048]{0:T(1024)} %select_n.50.source_ref, s32[2,4]{1,0:T(2,128)} %order_ref.3, f32[864,1024]{1,0:T(8,128)} %bitcast.3, f32[1,1024]{1,0:T(1,128)} %bitcast.4, f32[8,128]{1,0:T(8,128)} %wind_speed_ref.1, f32[8,128]{1,0:T(8,128)} %wind_dir_ref.1, ...), custom_call_target="tpu_custom_call" | custom-call | tf_op jit(solution)/shard_map/wave_sweeps/pallas_call | solution.py:592
  111.8 0.0 copy-done.2
  111.8 0.0 copy-start
  111.9 1.5 %copy-done = f32[432,8,128]{2,1,0:T(8,128)S(1)} copy-done((f32[432,8,128]{2,1,0:T(8,128)S(1)}, f32[432,8,128]{2,1,0:T(8,128)}, u32[]{:S(2)}) %copy-start) | copy-done | bytes 1769496
  113.3 0.0 copy-start.1
  113.3 1.5 %copy-done.1 = f32[432,8,128]{2,1,0:T(8,128)S(1)} copy-done((f32[432,8,128]{2,1,0:T(8,128)S(1)}, f32[432,8,128]{2,1,0:T(8,128)}, u32[]{:S(2)}) %copy-start.1) | copy-done | bytes 1769496
  114.8 6.0 %join_cores.1 = f32[864,8,128]{2,1,0:T(8,128)} custom-call(s32[2,4]{1,0:T(2,128)S(1)} %copy-done.2, f32[432,8,128]{2,1,0:T(8,128)S(1)} %copy-done, f32[432,8,128]{2,1,0:T(8,128)S(1)} %copy-done.1), custom_call_target="tpu_custom_call" | custom-call | tf_op jit(solution)/shard_map/join_cores/pallas_call | solution.py:706
  (1 shorter events, 0.0 us)
Async XLA Ops:
  1.3 110.5 %copy-start.2 = (s32[2,4]{1,0:T(2,128)S(1)}, s32[2,4]{1,0:T(2,128)}, u32[]{:S(2)}) copy-start(s32[2,4]{1,0:T(2,128)} %order_ref.3) | copy-start | bytes 100
  111.8 1.5 %copy-start = (f32[432,8,128]{2,1,0:T(8,128)S(1)}, f32[432,8,128]{2,1,0:T(8,128)}, u32[]{:S(2)}) copy-start(f32[432,8,128]{2,1,0:T(8,128)} %get-tuple-element.7.keep_ref) | copy-start | bytes 5308420
  113.3 1.5 %copy-start.1 = (f32[432,8,128]{2,1,0:T(8,128)S(1)}, f32[432,8,128]{2,1,0:T(8,128)}, u32[]{:S(2)}) copy-start(f32[432,8,128]{2,1,0:T(8,128)} %get-tuple-element.8.got_ref) | copy-start | bytes 5308420

commit v5 on v4

--- a/solution.py
+++ b/solution.py
@@ -532,8 +532,8 @@
     sums(3)
     sums(4)
     sums(5)
+    spread_out(0)
     sums(6)
-    spread_out(0)
     spread_out(1)
     first_sweep(0)
     spread_out(2)
@@ -677,42 +677,60 @@
     return source, rim.astype(jnp.float32)[None]
 
 
-def join_kernel(order_ref, keep_ref, got_ref, out_ref):
+def join_kernel(
+    order_ref, keep_ref, got_ref, out_ref, mine_ref, theirs_ref, done_ref, load_sem, save_sem
+):
     core = lax.axis_index("rows")
-    half = pl.program_id(2)
-    lane = lax.broadcasted_iota(jnp.int32, out_ref.shape, 2)
-    mine = lane // HALF == core
-
-    @pl.when(half == core)
-    def _():
-        out_ref[...] = jnp.where(mine, keep_ref[...], pltpu.roll(got_ref[...], HALF, 2))
-
-    @pl.when(half != core)
-    def _():
-        out_ref[...] = jnp.where(mine, pltpu.roll(keep_ref[...], HALF, 2), got_ref[...])
+    part = KQ // 2
+    loads = []
+    for index in range(4):
+        rows = pl.ds(index * part, part)
+        pair_of_copies = (
+            pltpu.make_async_copy(keep_ref.at[rows], mine_ref.at[rows], load_sem.at[index, 0]),
+            pltpu.make_async_copy(got_ref.at[rows], theirs_ref.at[rows], load_sem.at[index, 1]),
+        )
+        for copy in pair_of_copies:
+            copy.start()
+        loads.append(pair_of_copies)
+    lane = lax.broadcasted_iota(jnp.int32, (part,) + out_ref.shape[1:], 2)
+    at_home = lane // HALF == core
+    saves = []
+    for index in range(4):
+        for copy in loads[index]:
+            copy.wait()
+        mine = mine_ref[index * part : (index + 1) * part]
+        theirs = theirs_ref[index * part : (index + 1) * part]
+        as_is = jnp.where(at_home, mine, pltpu.roll(theirs, HALF, 2))
+        turned = jnp.where(at_home, pltpu.roll(mine, HALF, 2), theirs)
+        for half in range(2):
+            slot = 2 * index + half
+            done_ref[slot] = jnp.where(core == half, as_is, turned)
+            start = order_ref[ITERS - 1, index // 2 * 2 + half] * KQ + index % 2 * part
+            save = pltpu.make_async_copy(
+                done_ref.at[slot], out_ref.at[pl.ds(start, part)], save_sem.at[slot]
+            )
+            save.start()
+            saves.append(save)
+    for save in saves:
+        save.wait()
 
 
 def join(order, keep, got):
-    parts = 3
     rows, lanes = keep.shape[1:]
-    block = (KQ // parts, rows, lanes)
-
-    def pair_of(pair, part, half, order_ref):
-        return (pair * parts + part, 0, 0)
-
-    def quad_of(pair, part, half, order_ref):
-        return (order_ref[ITERS - 1, pair * 2 + half] * parts + part, 0, 0)
-
+    anywhere = pl.BlockSpec(memory_space=pl.ANY)
     return pl.pallas_call(
         join_kernel,
         out_shape=jax.ShapeDtypeStruct((K, rows, lanes), jnp.float32),
-        grid_spec=pltpu.PrefetchScalarGridSpec(
-            num_scalar_prefetch=1,
-            grid=(2, parts, 2),
-            in_specs=[pl.BlockSpec(block, pair_of), pl.BlockSpec(block, pair_of)],
-            out_specs=pl.BlockSpec(block, quad_of),
-        ),
-        compiler_params=pltpu.CompilerParams(vmem_limit_bytes=24 << 20),
+        in_specs=[pl.BlockSpec(memory_space=pltpu.SMEM), anywhere, anywhere],
+        out_specs=anywhere,
+        scratch_shapes=[
+            pltpu.VMEM(keep.shape, jnp.float32),
+            pltpu.VMEM(got.shape, jnp.float32),
+            pltpu.VMEM((8, KQ // 2, rows, lanes), jnp.float32),
+            pltpu.SemaphoreType.DMA((4, 2)),
+            pltpu.SemaphoreType.DMA((8,)),
+        ],
+        compiler_params=pltpu.CompilerParams(vmem_limit_bytes=60 << 20),
         name="join_cores",
     )(order, keep, got)
 

time: 121 us -> 115 us (0.950)
  Pallas kernels: 114 us -> 111 us
  local copies, waits for them, and re-layouts: 3.74 us -> 0.79 us
    unnamed x6 -> x0, local copies, waits for them, and re-layouts: 2.95 us -> none
    pallas_call x1, Pallas kernels: 108 us -> 106 us  [wave_sweeps(): pl.pallas_call(wave_kernel, out_shape=(jax.ShapeDtypeStruct((2 * KQ, ROWS...]
    pallas_call x1, Pallas kernels: 5.99 us -> 4.2 us  [join(): pl.pallas_call(join_kernel, out_shape=jax.ShapeDtypeStruct((K, rows, lane...]
where the time goes in v5:
time: 115 us; the launch traced here: 114 us
  Pallas kernels  111 us (97%)
  matrix products  1.46 us (1%)
  other arithmetic  1.31 us (1%)
    pallas_call x1, Pallas kernels, wave_sweeps(): pl.pallas_call(wave_kernel, out_shape=(jax.ShapeDtypeStruct((2 * KQ, ROWS...  106 us
    pallas_call x1, Pallas kernels, join(): pl.pallas_call(join_kernel, out_shape=jax.ShapeDtypeStruct((K, rows, lane...  4.2 us

profile of v5, /device:TPU:1, one launch (start us, length us, event | category | flops | bytes accessed | tf_op | source)
XLA Modules:
  0.0 114.3 jit_solution(14221067911889232168)
XLA Ops:
  0.0 1.3 %fusion.14 = (f32[1024]{0:T(1024)}, s32[1024]{0:T(1024)S(1)}, f32[1024]{0:T(1024)S(1)}) fusion(s32[1024]{0:T(1024)} %param.18), kind=kLoop, calls=%fused_computation.32 | loop fusion | flops 68608 | bytes 16384 | tf_op jit(solution)/shard_map/convert_element_type | solution.py:677
  1.3 0.6 fusion.2
  1.9 0.8 add_select_fusion
  2.8 0.1 copy.14
  2.9 0.7 select_n.50.source_ref
  3.6 106.4 %wave_sweeps.1 = (f32[432,8,128]{2,1,0:T(8,128)}, f32[432,8,128]{2,1,0:T(8,128)}) custom-call(s32[2048]{0:T(1024)} %select_n.50.source_ref, s32[2,4]{1,0:T(2,128)} %order_ref.3, f32[864,1024]{1,0:T(8,128)} %bitcast.3, f32[1,1024]{1,0:T(1,128)} %bitcast.4, f32[8,128]{1,0:T(8,128)} %wind_speed_ref.1, f32[8,128]{1,0:T(8,128)} %wind_dir_ref.1, ...), custom_call_target="tpu_custom_call" | custom-call | tf_op jit(solution)/shard_map/wave_sweeps/pallas_call | solution.py:592
  110.0 4.2 %join_cores.1 = f32[864,8,128]{2,1,0:T(8,128)} custom-call(s32[2,4]{1,0:T(2,128)} %order_ref.3, f32[432,8,128]{2,1,0:T(8,128)} %get-tuple-element.7.keep_ref, f32[432,8,128]{2,1,0:T(8,128)} %get-tuple-element.8.got_ref), custom_call_target="tpu_custom_call" | custom-call | tf_op jit(solution)/shard_map/join_cores/pallas_call | solution.py:721
  (1 shorter events, 0.0 us)
